TPU v7x, 256 devices: a whole 4x4x8 slice. The times are simulated.
256 devices in a mesh: seq: 8 (over y, core), users: 32 (over x, z).
Axes of the slice: x: 4, y: 4, z: 8, core: 2. Of those that a mesh axis runs over, the one named last changes fastest.
Arguments:
- hidden: float32 [32, 8192, 512], P('users', 'seq'), may hold values from -256 to 256
- target: bfloat16 [32, 8192, 512], P('users', 'seq'), may hold values from -0.25 to 0.25
- pool_table: bfloat16 [8192, 512], P('users'), may hold values from -1 to 1
- pool_items: int32 [8192], P('users'), may hold values from 1 to 16383
- labels: int32 [32, 8192], P('users', 'seq'), may hold values from 1 to 16383
- chosen: int32 [32, 64, 8], P('users', 'seq'), may hold values from 0 to 31, all different within a row
- offsets: int32 [32, 5], P('users'), may hold values from 0 to 8192, as said below
Outputs:
- loss: float32 [], replicated
- grad_hidden: float32 [32, 8192, 512], P('users', 'seq')
- grad_table: float32 [8192, 512], P('users')
Inputs may be any that keep to these rules, and one draw needn't show every extreme that they name: Each row offsets[u] starts at 0 and rises strictly; its last entry is the number of live positions of group u, and equals 8192 in some group; positions from it on are padding. `chosen`: each position block names 8 different negative blocks.
All inputs are finite; a program needn't handle non-finite values.
Results may differ from a plain program's by a relative error of at most 0.003.
Values may be sent and summed in bfloat16 or wider, within the bound.
A program may use at most 192 MiB of HBM per device.

v0:
```python
import jax
import jax.numpy as jnp
from jax import lax
from jax.sharding import PartitionSpec as P

NB = 256
PB = 128


def history_weights(bounds, positions):
    starts = bounds[:-1]
    finish = bounds[1:]
    lengths = (finish - starts).astype(jnp.float32)
    inside = (positions[..., None] >= starts) & (positions[..., None] < finish)
    return jnp.sum(jnp.where(inside, 1.0 / lengths, 0.0), axis=-1)


def block_terms(states, target, labels, weights, chosen, pool_rows, pool_ids, factor):
    narrow = states.astype(jnp.bfloat16)
    negatives = jnp.take(pool_rows, chosen, axis=0).reshape(-1, pool_rows.shape[2])
    neg_items = jnp.take(pool_ids, chosen, axis=0).reshape(-1)
    scores = jnp.dot(narrow, negatives.T, preferred_element_type=jnp.float32)
    target_wide = target.astype(jnp.float32)
    positive = jnp.sum(narrow.astype(jnp.float32) * target_wide, axis=1)
    masked = jnp.where(neg_items[None, :] == labels[:, None], -1e30, scores)
    peak = jnp.maximum(positive, jnp.max(masked, axis=1))
    neg_exp = jnp.exp(masked - peak[:, None])
    pos_exp = jnp.exp(positive - peak)
    totals = pos_exp + jnp.sum(neg_exp, axis=1)
    cross = peak + jnp.log(totals) - positive
    coeff = weights * factor
    neg_grad = (coeff[:, None] * neg_exp / totals[:, None]).astype(jnp.bfloat16)
    pos_grad = coeff * (pos_exp / totals - 1.0)
    state_grad = (
        jnp.dot(neg_grad, negatives, preferred_element_type=jnp.float32)
        + pos_grad[:, None] * target_wide
    )
    pool_grad = jnp.dot(neg_grad.T, narrow, preferred_element_type=jnp.float32)
    pool_grad = pool_grad.reshape(chosen.shape[0], pool_rows.shape[1], pool_rows.shape[2])
    return (jnp.sum(weights * cross), state_grad, pool_grad)


def run_blocks(
    states,
    targets,
    label_rows,
    weights,
    picked,
    visit_order,
    live_count,
    pool_rows,
    pool_ids,
    factor,
):
    batched = jax.vmap(block_terms, in_axes=(0, 0, 0, 0, 0, None, None, None))
    rounds = (live_count + 3) // 4

    def advance(turn_index, carried):
        loss_acc, grad_acc, state_acc = carried
        slot_picks = lax.dynamic_slice_in_dim(visit_order, turn_index * 4, 4)
        picked_now = jnp.take(picked, slot_picks, axis=0)
        part_loss, state_grad, pool_grad = batched(
            jnp.take(states, slot_picks, axis=0),
            jnp.take(targets, slot_picks, axis=0),
            jnp.take(label_rows, slot_picks, axis=0),
            jnp.take(weights, slot_picks, axis=0),
            picked_now,
            pool_rows,
            pool_ids,
            factor,
        )
        grad_acc = grad_acc.at[picked_now.reshape(-1)].add(
            pool_grad.reshape((-1,) + pool_grad.shape[2:])
        )
        state_acc = state_acc.at[slot_picks].set(state_grad)
        return (loss_acc + jnp.sum(part_loss), grad_acc, state_acc)

    initial = (
        jnp.zeros((), jnp.float32),
        jnp.zeros(pool_rows.shape, jnp.float32),
        jnp.zeros(states.shape, jnp.float32),
    )
    return lax.fori_loop(0, rounds, advance, initial)


def per_device(hidden, target, pool_table, pool_items, labels, chosen, offsets):
    user_count = lax.axis_size("users")
    length = hidden.shape[1]
    features = hidden.shape[2]
    block_count = length // PB
    shard_rows, shard_items = (
        lax.all_gather(pool_table, "users", axis=0, tiled=True),
        lax.all_gather(pool_items, "users", axis=0, tiled=True),
    )
    pool_rows = shard_rows.reshape(-1, NB, features)
    pool_ids = shard_items.reshape(-1, NB)
    factor = 1.0 / (user_count * (offsets.shape[1] - 1))
    seq_place = lax.axis_index("seq")
    live_blocks = (offsets[0, -1] + PB - 1) // PB
    states = hidden.reshape(block_count, PB, features)
    targets = target.reshape(block_count, PB, features)
    label_rows = labels.reshape(block_count, PB)
    picked = chosen.reshape(block_count, chosen.shape[2])
    within = jnp.arange(PB, dtype=jnp.int32)
    slot_index = jnp.arange(block_count, dtype=jnp.int32)
    positions = seq_place * length + slot_index[:, None] * PB + within[None, :]
    weights = history_weights(offsets[0], positions)
    live_count = jnp.clip(live_blocks - seq_place * block_count, 0, block_count)
    loss_part, grad_pool, state_grad = run_blocks(
        states,
        targets,
        label_rows,
        weights,
        picked,
        slot_index,
        live_count,
        pool_rows,
        pool_ids,
        factor,
    )
    grad_hidden = state_grad.reshape(hidden.shape)
    loss_total = lax.psum(loss_part, ("seq", "users")) * factor
    grad_full = grad_pool.reshape(-1, features)
    owned_rows = lax.psum_scatter(grad_full, "users", scatter_dimension=0, tiled=True)
    grad_table = lax.psum(owned_rows, "seq")
    return (loss_total, grad_hidden, grad_table)


def solution(mesh):
    return jax.shard_map(
        per_device,
        mesh=mesh,
        in_specs=(
            P("users", "seq", None),
            P("users", "seq", None),
            P("users", None),
            P("users"),
            P("users", "seq"),
            P("users", "seq", None),
            P("users", None),
        ),
        out_specs=(P(), P("users", "seq", None), P("users", None)),
        check_vma=False,
    )
```

profile of v0, /device:TPU:1, one launch (start us, length us, event | category | flops | bytes accessed | tf_op | source)
XLA Modules:
  0.0 614.7 jit_solution(12936901382694185869)
XLA Ops:
  9.9 38.2 %all-gather = s32[32,1,256]{2,1,0:T(1,128)S(1)} all-gather(s32[1,1,256]{2,1,0:T(1,128)} %bitcast.72), channel_id=1, replica_groups=mesh['seq'=8,'users'=32] {'users'}, dimensions={0}, use_global_device_ids=true | all-gather | bytes 33792 | tf_op jit(solution)/shard_map/all_gather | solution.py:93
  51.7 59.8 %all-gather.3.cloned.1.call-done = bf16[8192,512]{1,0:T(8,128)(2,1)} async-done(((bf16[256,512]{1,0:T(8,128)(2,1)}), bf16[8192,512]{1,0:T(8,128)(2,1)}) %all-gather.3.cloned.1.call-update) | async-done | bytes 8388624 | tf_op jit(solution)/shard_map/all_gather | solution.py:92
  113.1 7.9 %broadcast_in_dim.126 = f32[32,256,512]{2,1,0:T(8,128)} broadcast(f32[]{:T(128)} %copy.36), dimensions={} | broadcast | bytes 16777220 | tf_op jit(solution)/shard_map/broadcast_in_dim | solution.py:80
  120.9 163.8 %while.16 = (s32[]{:T(128)}, f32[]{:T(128)}, f32[32,256,512]{2,1,0:T(8,128)}, f32[8,128,512]{2,1,0:T(8,128)}, s32[]{:T(128)}, /*index=5*/s32[8]{0:T(128)S(1)}, f...) while((s32[]{:T(128)}, f32[]{:T(128)}, ...), condition=%wide.region_8.9_spmd, body=%wide.region_1.8_spmd.sunk | while | flops 3252174336 | bytes 194429456 | solution.py:83
  123.9 1.8 gather_fusion
  126.6 8.4 %gather_fusion.5 = bf16[32,256,512]{2,1,0:T(8,128)(2,1)} fusion(bf16[32,256,512]{2,1,0:T(8,128)(2,1)} %get-tuple-element.362, s32[1024]{0:T(1024)S(1)} %pad_clamp_fusion.5), kind=kCustom, calls=%fused_computation.6.clone.1 | custom fusion | bytes 16777344 | tf_op jit(solution)/shard_map/while/body/vmap(jit(_take))/gather | solution.py:20
  135.0 4.7 bitcast_select_fusion.3
  139.7 2.9 fusion.24
  142.9 1.9 copy-done
  147.0 6.5 %convolution_add_fusion.2 = f32[4,128,512]{2,1,0:T(8,128)S(1)} fusion(bf16[4,2048,512]{2,1,0:T(8,128)(2,1)} %copy-done.1, f32[4,128]{1,0:T(4,128)S(1)} %get-tuple-element.315, bf16[4,128,512]{2,1,0:T(8,128)(2,1)S(1)} %gather_fusion, pred[4]{0:T(512)(128)(4,1)S(1)} %get-tuple-element.305, f32[4,128,2048]{2,1,0:T(8,128)} %copy-done, ...), kind=kOutput, calls=%fused_computation.17.clone.1 | convolution fusion | flops 1081081856 | bytes 14198788 | tf_op jit(solution)/shard_map/while/body/vmap()/dot_general | solution.py:35
  153.5 2.8 scatter_fusion.1
  156.2 10.4 %fusion.27 = f32[4,2048,512]{2,1,0:T(8,128)} fusion(bf16[4,128,512]{2,1,0:T(8,128)(2,1)S(1)} %get-tuple-element.308, f32[4,128,2048]{2,1,0:T(8,128)} %copy-done, f32[4,128]{1,0:T(4,128)S(1)} %get-tuple-element.313, f32[4,128]{1,0:T(4,128)S(1)} %get-tuple-element.314, f32[4,128]{1,0:T(4,128)S(1)} %max.31, s32[4,128]{1,0:T(4,128)S(1)} %broadcast_select_fusion.7, ...), kind=kOutput, calls=%fused_computation.40.clone.1 | convolution fusion | flops 1080033280 | bytes 21536768 | tf_op jit(solution)/shard_map/while/body/vmap()/dot_general | solution.py:38
  166.7 36.2 %scatter_fusion = f32[32,256,512]{2,1,0:T(8,128)} fusion(f32[32,256,512]{2,1,0:T(8,128)} %get-tuple-element.335, s32[32]{0:T(128)S(1)} %fusion.26, f32[32,256,512]{2,1,0:T(8,128)} %bitcast.60), kind=kCustom, calls=%fused_computation.7.clone.1 | custom fusion | flops 4194304 | bytes 50331776 | tf_op jit(solution)/shard_map/while/body/scatter-add | solution.py:72
  208.6 8.4 %gather_fusion.5 = bf16[32,256,512]{2,1,0:T(8,128)(2,1)} fusion(bf16[32,256,512]{2,1,0:T(8,128)(2,1)} %get-tuple-element.362, s32[1024]{0:T(1024)S(1)} %pad_clamp_fusion.5), kind=kCustom, calls=%fused_computation.6.clone.1 | custom fusion | bytes 16777344 | tf_op jit(solution)/shard_map/while/body/vmap(jit(_take))/gather | solution.py:20
  217.0 4.7 bitcast_select_fusion.3
  221.6 2.9 fusion.24
  224.9 1.9 copy-done
  229.0 6.5 %convolution_add_fusion.2 = f32[4,128,512]{2,1,0:T(8,128)S(1)} fusion(bf16[4,2048,512]{2,1,0:T(8,128)(2,1)} %copy-done.1, f32[4,128]{1,0:T(4,128)S(1)} %get-tuple-element.315, bf16[4,128,512]{2,1,0:T(8,128)(2,1)S(1)} %gather_fusion, pred[4]{0:T(512)(128)(4,1)S(1)} %get-tuple-element.305, f32[4,128,2048]{2,1,0:T(8,128)} %copy-done, ...), kind=kOutput, calls=%fused_computation.17.clone.1 | convolution fusion | flops 1081081856 | bytes 14198788 | tf_op jit(solution)/shard_map/while/body/vmap()/dot_general | solution.py:35
  235.4 2.8 scatter_fusion.1
  238.2 10.4 %fusion.27 = f32[4,2048,512]{2,1,0:T(8,128)} fusion(bf16[4,128,512]{2,1,0:T(8,128)(2,1)S(1)} %get-tuple-element.308, f32[4,128,2048]{2,1,0:T(8,128)} %copy-done, f32[4,128]{1,0:T(4,128)S(1)} %get-tuple-element.313, f32[4,128]{1,0:T(4,128)S(1)} %get-tuple-element.314, f32[4,128]{1,0:T(4,128)S(1)} %max.31, s32[4,128]{1,0:T(4,128)S(1)} %broadcast_select_fusion.7, ...), kind=kOutput, calls=%fused_computation.40.clone.1 | convolution fusion | flops 1080033280 | bytes 21536768 | tf_op jit(solution)/shard_map/while/body/vmap()/dot_general | solution.py:38
  248.6 36.2 %scatter_fusion = f32[32,256,512]{2,1,0:T(8,128)} fusion(f32[32,256,512]{2,1,0:T(8,128)} %get-tuple-element.335, s32[32]{0:T(128)S(1)} %fusion.26, f32[32,256,512]{2,1,0:T(8,128)} %bitcast.60), kind=kCustom, calls=%fused_computation.7.clone.1 | custom fusion | flops 4194304 | bytes 50331776 | tf_op jit(solution)/shard_map/while/body/scatter-add | solution.py:72
  284.9 240.4 %reduce-scatter.2.cloned.1.call-done = f32[256,512]{1,0:T(8,128)} async-done(((f32[8192,512]{1,0:T(8,128)}), f32[256,512]{1,0:T(8,128)}) %reduce-scatter.2.cloned.1.call-update) | async-done | bytes 524304 | tf_op jit(solution)/shard_map/reduce_scatter | solution.py:124
  525.3 79.2 %psum.14 = f32[]{:T(128)} all-reduce(f32[]{:T(128)} %get-tuple-element.169), channel_id=1, replica_groups=mesh['seq'=8,'users'=32] {'seq','users'}, use_global_device_ids=true, to_apply=%region_9.10 | all-reduce | flops 1 | bytes 8 | tf_op jit(solution)/shard_map/psum | solution.py:122
  605.2 1.9 copy.37
  (72 shorter events, 20.6 us)
Async XLA Ops:
  7.2 104.3 %all-gather.3.cloned.1.call-start = ((), (), s32[]{:S(2)}) async-start(), calls=%async_computation.1 | async-start | bytes 8650752 | tf_op jit(solution)/shard_map/all_gather | solution.py:92
  7.9 517.4 %reduce-scatter.2.cloned.1.call-start = ((), (), s32[]{:S(2)}) async-start(), calls=%async_computation.2 | async-start | bytes 17301504 | tf_op jit(solution)/shard_map/reduce_scatter | solution.py:124
  113.1 7.9 %copy-start.2 = (s32[1,8,8]{2,1,0:T(8,128)S(1)}, s32[1,8,8]{2,1,0:T(8,128)}, u32[]{:S(2)}) copy-start(s32[1,8,8]{2,1,0:T(8,128)} %param.14) | copy-start | bytes 772
  113.1 7.9 %copy-start.3 = (s32[1,1024]{1,0:T(1,128)S(1)}, s32[1,1024]{1,0:T(1,128)}, u32[]{:S(2)}) copy-start(s32[1,1024]{1,0:T(1,128)} %param.13) | copy-start | bytes 12292
  139.7 3.2 copy-start.1
  142.9 1.9 copy-start
  221.6 3.2 copy-start.1
  224.9 1.9 copy-start
  284.8 320.4 %all-reduce.2.cloned.1.call-start = ((), (), s32[]{:S(2)}) async-start(), calls=%async_computation.3 | async-start | bytes 1048576 | tf_op jit(solution)/shard_map/psum | solution.py:125
Sparse Core Ops, SparseCore 0:
  10.6 100.8 all-gather.2
  284.9 240.3 reduce-scatter.1
  527.6 66.9 all-reduce.1
where the time goes:
time: 616 us; the launch traced here: 615 us
  waiting for transfers between devices  301 us (49%)
  blocking collectives  117 us (19%)
  other arithmetic  89.1 us (14%)
  local copies, waits for them, and re-layouts  50.1 us (8%)
  matrix products  39.5 us (6%)
  between operations  16.2 us (3%)
    reduce_scatter x1, waiting for transfers between devices, per_device(): lax.psum_scatter(grad_full, 'users', scatter_dimension=0, tiled=True)  240 us
    psum x1, blocking collectives, per_device(): loss_total = lax.psum(loss_part, ('seq', 'users')) * factor  79.2 us
    scatter-add x2, other arithmetic, advance(): grad_acc.at[picked_now.reshape(-1)]  72.4 us
    all_gather x1, waiting for transfers between devices, per_device(): lax.all_gather(pool_table, 'users', axis=0, tiled=True)  59.8 us
    all_gather x1, blocking collectives, per_device(): lax.all_gather(pool_items, 'users', axis=0, tiled=True)  38.2 us
    dot_general x2, matrix products, block_terms(): pool_grad = jnp.dot(neg_grad.T, narrow, preferred_element_type=jnp.float32)  20.9 us
    gather x2, local copies, waits for them, and re-layouts, block_terms(): jnp.take(pool_rows, chosen, axis=0).reshape(-1, pool_rows.shape[2])  16.7 us
    dot_general x2, matrix products, block_terms(): jnp.dot(neg_grad, negatives, preferred_element_type=jnp.float32)  12.9 us
  transfers between devices with their start and end apart: 3, of which 2 were waited for; matrix products, arithmetic and copies ran while one was open for 1% of the time, Pallas kernels for 0%

commit v1 on v0

v1 whole, which is shorter than its diff:
```python
import functools
import jax
import jax.numpy as jnp
from jax import lax
from jax.experimental import pallas as pl
from jax.experimental.pallas import tpu as pltpu
from jax.sharding import PartitionSpec as P

MESH = pl.DeviceIdType.MESH
NX, NY, NZ = 4, 4, 8


def where_am_i():
    seq, users = lax.axis_index("seq"), lax.axis_index("users")
    return users // NZ, seq // 2, users % NZ, seq % 2


def device(x, y, z, c):
    return {"seq": y * 2 + c, "users": x * NZ + z}


def greet(peers):
    barrier = pltpu.get_barrier_semaphore()
    for peer in peers:
        pl.semaphore_signal(barrier, inc=1, device_id=peer, device_id_type=MESH)
    pl.semaphore_wait(barrier, len(peers))


def push(src, dst, send_sem, recv_sem, to):
    copy = pltpu.make_async_remote_copy(src_ref=src, dst_ref=dst, send_sem=send_sem, recv_sem=recv_sem,
                                        device_id=to, device_id_type=MESH)
    copy.start()
    return copy


def gather_kernel(shard, items, table, all_items, local_sem, partner_send, partner_recv, item_send, item_recv,
                  send1, recv1, send2, recv2):
    x, y, z, c = where_am_i()
    users = x * NZ + z
    total = NX * NZ
    quarter = shard.shape[1] // 2
    others = [lax.rem(users + d, total) for d in range(1, total)]
    partner = device(x, y, z, 1 - c)
    greet([{"seq": y * 2 + c, "users": u} for u in others] + [partner])

    mine = pltpu.make_async_copy(shard, table.at[users], local_sem.at[0])
    mine.start()
    mine_items = pltpu.make_async_copy(items, all_items.at[users], local_sem.at[1])
    mine_items.start()

    def run(n1, n2, me1, me2, region, dev):
        copies, pending = [], {}

        def part(ref, s, n, d):
            return ref if s < n // 2 else ref.at[pl.ds(0 if d > 0 else quarter, quarter)]

        def size(ring):
            return n1 if ring == 1 else n2

        def place(ring, sub, back):
            if ring == 1:
                return lax.rem(me1 - back + n1, n1), me2
            return lax.rem(me1 + sub + n1, n1), lax.rem(me2 - back + n2, n2)

        def send(ring, sub, s, d):
            n = size(ring)
            dst = region(*place(ring, sub, d * (s - 1)))
            src = shard.at[c] if s == 1 and sub == 0 else dst
            if ring == 1:
                k = (s - 1) * 2 + (d < 0)
                sems, to = (send1.at[k], recv1.at[k]), dev(lax.rem(me1 + d + n, n), me2)
            else:
                k = ((sub % n1) * (n2 // 2) + s - 1) * 2 + (d < 0)
                sems, to = (send2.at[k], recv2.at[k]), dev(me1, lax.rem(me2 + d + n, n))
            copy = push(part(src, s, n, d), part(dst, s, n, d), *sems, to)
            copies.append(copy)
            pending[ring, sub, s, d] = copy

        passed = []

        def arrive(ring, sub, s, d):
            pending.pop((ring, sub, s, d)).wait_recv()
            ref = part(region(*place(ring, sub, d * s)), s, size(ring), d)
            passed.append(push(ref, ref, partner_send.at[len(passed)], partner_recv, partner))

        ready = {0: 0}
        for s in range(1, n1 // 2):
            ready[-s], ready[s] = s, s
        ready[n1 // 2] = n1 // 2
        for time in range(1, n1 // 2 + n2 // 2 + 2):
            if time <= n1 // 2 + 1:
                for d in (1, -1):
                    if time > 1:
                        arrive(1, 0, time - 1, d)
                    if time <= n1 // 2:
                        send(1, 0, time, d)
            for sub, at in ready.items():
                s = time - at
                if 1 <= s <= n2 // 2 + 1:
                    for d in (1, -1):
                        if s > 1:
                            arrive(2, sub, s - 1, d)
                        if s <= n2 // 2:
                            send(2, sub, s, d)
        assert not pending
        for copy in copies + passed:
            copy.wait_send()

    shared = [push(items, all_items.at[users], item_send.at[d], item_recv, {"seq": y * 2 + c, "users": u})
              for d, u in enumerate(others)]

    @pl.when(c == 0)
    def _():
        run(NX, NZ, x, z, lambda i1, i2: table.at[i1 * NZ + i2, 0], lambda i1, i2: device(i1, y, i2, 0))

    @pl.when(c == 1)
    def _():
        run(NZ, NX, z, x, lambda i1, i2: table.at[i2 * NZ + i1, 1], lambda i1, i2: device(i2, y, i1, 1))

    for copy in shared:
        copy.wait_send()
    rest = all_items.at[pl.ds(0, total - 1)]
    pltpu.make_async_copy(rest, rest, item_recv).wait()
    rest = table.at[pl.ds(0, total - 1), 0]
    pltpu.make_async_copy(rest, rest, partner_recv).wait()
    mine.wait()
    mine_items.wait()


def gather(pool_table, pool_items):
    rows, features = pool_table.shape
    total = NX * NZ
    dma = pltpu.SemaphoreType.DMA
    anywhere = pl.BlockSpec(memory_space=pl.ANY)
    table, items = pl.pallas_call(
        gather_kernel,
        in_specs=[pl.BlockSpec(memory_space=pltpu.VMEM)] * 2,
        out_specs=[anywhere, anywhere],
        out_shape=(
            jax.ShapeDtypeStruct((total, 2, rows // 2, features), pool_table.dtype),
            jax.ShapeDtypeStruct((total, 1, rows), pool_items.dtype),
        ),
        scratch_shapes=[dma((2,)), dma((40,)), dma, dma((total - 1,)), dma, dma((8,)), dma((8,)), dma((32,)),
                        dma((32,))],
        compiler_params=pltpu.CompilerParams(collective_id=0, has_side_effects=True),
        name="gather",
    )(pool_table.reshape(2, rows // 2, features), pool_items.reshape(1, rows))
    return table.reshape(total, rows, features), items


NB = 256
PB = 128


def score_kernel(chosen_s, offsets_s, place_s, hidden_ref, target_ref, labels_ref, table_ref, items_ref,
                 gh_ref, loss_ref, gt_hbm, acc, scores, grads, loss_acc, sem, *, factor):
    b = pl.program_id(0)
    blocks = pl.num_programs(0)
    features = hidden_ref.shape[1]
    kb = chosen_s.shape[1]
    hists = offsets_s.shape[0] - 1
    base = place_s[0] + b * PB

    @pl.when(b == 0)
    def _():
        loss_acc[...] = jnp.zeros_like(loss_acc)

        @pl.loop(0, acc.shape[0])
        def _(k):
            acc[k] = jnp.zeros(acc.shape[1:], acc.dtype)

    live = base < offsets_s[hists]

    @pl.when(jnp.logical_not(live))
    def _():
        gh_ref[...] = jnp.zeros_like(gh_ref)

    @pl.when(live)
    def _():
        narrow = hidden_ref[...].astype(jnp.bfloat16)
        target_wide = target_ref[...].astype(jnp.float32)
        positive = jnp.sum(narrow.astype(jnp.float32) * target_wide, axis=1, keepdims=True)
        labels = jnp.broadcast_to(labels_ref[0], (PB, PB)).T[:, :1]
        positions = base + lax.broadcasted_iota(jnp.int32, (PB, 1), 0)
        weights = jnp.zeros((PB, 1), jnp.float32)
        for h in range(hists):
            start, finish = offsets_s[h], offsets_s[h + 1]
            length = jnp.broadcast_to(finish - start, (PB, 1)).astype(jnp.float32)
            inside = (positions >= start) & (positions < finish)
            weights = weights + jnp.where(inside, 1.0 / length, 0.0)

        top = jnp.full((PB, 128), -1e30, jnp.float32)
        for j in range(kb):
            k = chosen_s[b, j]
            raw = lax.dot_general(narrow, table_ref[k], (((1,), (1,)), ((), ())),
                                  preferred_element_type=jnp.float32)
            masked = jnp.where(items_ref[k] == labels, -1e30, raw)
            scores[:, j * NB:(j + 1) * NB] = masked
            for i in range(NB // 128):
                top = jnp.maximum(top, masked[:, i * 128:(i + 1) * 128])
        peak = jnp.maximum(positive, jnp.max(top, axis=1, keepdims=True))
        added = jnp.zeros((PB, 128), jnp.float32)
        for j in range(kb):
            each = jnp.exp(scores[:, j * NB:(j + 1) * NB] - peak)
            scores[:, j * NB:(j + 1) * NB] = each
            for i in range(NB // 128):
                added = added + each[:, i * 128:(i + 1) * 128]
        pos_exp = jnp.exp(positive - peak)
        totals = pos_exp + jnp.sum(added, axis=1, keepdims=True)
        cross = peak + jnp.log(totals) - positive
        loss_acc[...] += jnp.broadcast_to(jnp.sum(weights * cross, axis=0, keepdims=True), loss_acc.shape)
        coeff = weights * factor
        scale = coeff / totals
        pos_grad = coeff * (pos_exp / totals - 1.0)
        for j in range(kb):
            grads[:, j * NB:(j + 1) * NB] = (scores[:, j * NB:(j + 1) * NB] * scale).astype(jnp.bfloat16)
        out = pos_grad * target_wide
        for j in range(kb):
            k = chosen_s[b, j]
            g = grads[:, j * NB:(j + 1) * NB]
            out = out + jnp.dot(g, table_ref[k], preferred_element_type=jnp.float32)
            acc[k] += lax.dot_general(g, narrow, (((0,), (0,)), ((), ())), preferred_element_type=jnp.float32)
        gh_ref[...] = out

    @pl.when(b == blocks - 1)
    def _():
        loss_ref[...] = loss_acc[...]
        copy = pltpu.make_async_copy(acc, gt_hbm, sem)
        copy.start()
        copy.wait()


def score(hidden, target, labels, chosen, offsets, place, table, items, factor):
    rows, features = hidden.shape
    blocks = rows // PB
    count = table.shape[0]
    kb = chosen.shape[1]
    one = pl.Buffered(1)
    grid_spec = pltpu.PrefetchScalarGridSpec(
        num_scalar_prefetch=3,
        grid=(blocks,),
        in_specs=[
            pl.BlockSpec((PB, features), lambda b, *_: (b, 0)),
            pl.BlockSpec((PB, features), lambda b, *_: (b, 0)),
            pl.BlockSpec((1, 1, PB), lambda b, *_: (b, 0, 0)),
            pl.BlockSpec((count, NB, features), lambda b, *_: (0, 0, 0), pipeline_mode=one),
            pl.BlockSpec((count, 1, NB), lambda b, *_: (0, 0, 0), pipeline_mode=one),
        ],
        out_specs=[
            pl.BlockSpec((PB, features), lambda b, *_: (b, 0)),
            pl.BlockSpec((8, 128), lambda b, *_: (0, 0)),
            pl.BlockSpec(memory_space=pl.ANY),
        ],
        scratch_shapes=[
            pltpu.VMEM((count, NB, features), jnp.float32),
            pltpu.VMEM((PB, kb * NB), jnp.float32),
            pltpu.VMEM((PB, kb * NB), jnp.bfloat16),
            pltpu.VMEM((8, 128), jnp.float32),
            pltpu.SemaphoreType.DMA,
        ],
    )
    return pl.pallas_call(
        functools.partial(score_kernel, factor=factor),
        grid_spec=grid_spec,
        out_shape=(
            jax.ShapeDtypeStruct((rows, features), jnp.float32),
            jax.ShapeDtypeStruct((8, 128), jnp.float32),
            jax.ShapeDtypeStruct((count, NB, features), jnp.float32),
        ),
        compiler_params=pltpu.CompilerParams(vmem_limit_bytes=48 << 20),
        name="score",
    )(chosen, offsets, place, hidden, target, labels.reshape(blocks, 1, PB), table, items)


def reduce_kernel(grads, loss_in, out, loss_out, own, first, half_up, half_down, full_up, full_down,
                  chunk_half_up, chunk_half_down, chunk_up, chunk_down, tail_up, tail_down, parts, sums,
                  load_sem, pair_send, pair_recv, s1, r1, s2, r2, s3, r3, s4, r4, s5, r5, loss_send, loss_recv):
    x, y, z, c = where_am_i()
    me1 = y * (1 - c) + x * c
    me2 = x * (1 - c) + y * c
    partner = device(x, y, z, 1 - c)

    def dev(i1, i2, iz):
        return device(i2 * (1 - c) + i1 * c, i1 * (1 - c) + i2 * c, iz, c)

    xs = [device(lax.rem(x + d, NX), y, z, c) for d in range(1, NX)]
    ys = [device(x, lax.rem(y + d, NY), z, c) for d in range(1, NY)]
    zs = [device(x, y, lax.rem(z + d, NZ), c) for d in range(1, NZ)]
    greet([partner] + xs + ys + zs)
    sent = []

    def unit(core, i1, i2):
        return grads.at[i2 * (1 - core) + i1 * core, :, core, i1 * (1 - core) + i2 * core]

    order = [(2, 0), (2, 1), (1, 1), (3, 0), (1, 0), (3, 1), (0, 0), (0, 1)]
    other1 = x * (1 - c) + y * c
    pair, load = {}, {}
    slot = 0
    for d, h in order:
        for q in (2 * h, 2 * h + 1):
            p = lax.rem(other1 + d, 4)
            copy = push(unit(1 - c, p, q), first.at[p, q], pair_send.at[slot], pair_recv.at[slot], partner)
            sent.append(copy)
            p = lax.rem(me1 + d, 4)
            here = pltpu.make_async_copy(unit(c, p, q), own.at[p, q], load_sem.at[slot])
            here.start()
            pair[d, q], load[d, q] = copy, here
            slot += 1

    def loss_round(k, base, count, me, peers):
        parts[base + me] = sums[...]
        copies = []
        for d, peer in enumerate(peers):
            copies.append(push(sums, parts.at[base + me], loss_send.at[k + d], loss_recv.at[k + d], peer))
        return copies

    def loss_sum(copies, base, count):
        for copy in copies:
            copy.wait()
        total = parts[base]
        for i in range(1, count):
            total = total + parts[base + i]
        sums[...] = total

    sums[...] = loss_in[...]
    rounds = loss_round(0, 0, 2, c, [partner])

    def together(d, h):
        p = lax.rem(me1 + d, 4)
        for q in (2 * h, 2 * h + 1):
            pair[d, q].wait_recv()
            load[d, q].wait()

            @pl.loop(0, NZ)
            def _(i):
                own[p, q, i] += first[p, q, i]

    def add(dst, src, count):
        @pl.loop(0, count)
        def _(i):
            dst[i] += src[i]

    up1, down1 = dev(lax.rem(me1 + 1, 4), me2, z), dev(lax.rem(me1 + 3, 4), me2, z)
    opposite, above, below = lax.rem(me1 + 2, 4), lax.rem(me1 + 1, 4), lax.rem(me1 + 3, 4)

    def half(ref, h, size):
        return ref.at[pl.ds(h * size, size)]

    together(2, 0)
    a_up = push(half(own.at[opposite], 0, 2), half_up, s1.at[0], r1.at[0], up1)
    together(2, 1)
    a_down = push(half(own.at[opposite], 1, 2), half_down, s1.at[1], r1.at[1], down1)
    together(1, 1)
    b_up = push(half(own.at[above], 1, 2), half(full_up, 1, 2), s1.at[2], r1.at[2], up1)
    together(3, 0)
    b_down = push(half(own.at[below], 0, 2), half(full_down, 0, 2), s1.at[3], r1.at[3], down1)
    together(1, 0)
    together(3, 1)

    def add_units(p, h, ref, base):
        for q in range(2):
            @pl.loop(0, NZ)
            def _(i):
                own[p, 2 * h + q, i] += ref[base + q, i]

    a_up.wait_recv()
    add_units(above, 0, half_up, 0)
    c_up = push(half(own.at[above], 0, 2), half(full_up, 0, 2), s1.at[4], r1.at[4], up1)
    a_down.wait_recv()
    add_units(below, 1, half_down, 0)
    c_down = push(half(own.at[below], 1, 2), half(full_down, 1, 2), s1.at[5], r1.at[5], down1)
    sent += [a_up, a_down, b_up, b_down, c_up, c_down]
    together(0, 0)
    together(0, 1)
    loss_sum(rounds, 0, 2)
    rounds = loss_round(1, 2, NY, y, ys)
    b_up.wait_recv()
    add_units(me1, 1, full_up, 2)
    b_down.wait_recv()
    add_units(me1, 0, full_down, 0)
    c_up.wait_recv()
    add_units(me1, 0, full_up, 0)
    c_down.wait_recv()
    add_units(me1, 1, full_down, 2)

    mine = own.at[me1]
    up2, down2 = dev(me1, lax.rem(me2 + 1, 4), z), dev(me1, lax.rem(me2 + 3, 4), z)
    opposite, above, below = lax.rem(me2 + 2, 4), lax.rem(me2 + 1, 4), lax.rem(me2 + 3, 4)
    a_up = push(half(mine.at[opposite], 0, 4), chunk_half_up, s2.at[0], r2.at[0], up2)
    a_down = push(half(mine.at[opposite], 1, 4), chunk_half_down, s2.at[1], r2.at[1], down2)
    b_up = push(half(mine.at[above], 1, 4), half(chunk_up, 1, 4), s2.at[2], r2.at[2], up2)
    b_down = push(half(mine.at[below], 0, 4), half(chunk_down, 0, 4), s2.at[3], r2.at[3], down2)
    loss_sum(rounds, 2, NY)
    rounds = loss_round(4, 6, NX, x, xs)
    a_up.wait_recv()
    add(half(mine.at[above], 0, 4), chunk_half_up, 4)
    c_up = push(half(mine.at[above], 0, 4), half(chunk_up, 0, 4), s2.at[4], r2.at[4], up2)
    a_down.wait_recv()
    add(half(mine.at[below], 1, 4), chunk_half_down, 4)
    c_down = push(half(mine.at[below], 1, 4), half(chunk_down, 1, 4), s2.at[5], r2.at[5], down2)
    sent += [a_up, a_down, b_up, b_down, c_up, c_down]
    here = mine.at[me2]
    b_up.wait_recv()
    add(half(here, 1, 4), half(chunk_up, 1, 4), 4)
    b_down.wait_recv()
    add(half(here, 0, 4), half(chunk_down, 0, 4), 4)
    c_up.wait_recv()
    add(half(here, 0, 4), half(chunk_up, 0, 4), 4)
    c_down.wait_recv()
    add(half(here, 1, 4), half(chunk_down, 1, 4), 4)
    loss_sum(rounds, 6, NX)
    rounds = loss_round(7, 10, NZ, z, zs)

    up3, down3 = dev(me1, me2, lax.rem(z + 1, NZ)), dev(me1, me2, lax.rem(z + NZ - 1, NZ))
    rows = own.shape[3]
    for s in range(1, NZ // 2 + 1):
        ahead = NZ // 2 + 1 - s
        goes_up, goes_down = lax.rem(z + ahead, NZ), lax.rem(z + NZ - ahead, NZ)
        if s == 1:
            u_src, u_dst = half(here.at[goes_up], 0, rows // 2), half(tail_up.at[0], 0, rows // 2)
            d_src, d_dst = half(here.at[goes_down], 1, rows // 2), half(tail_down.at[0], 1, rows // 2)
        else:
            u_src, u_dst, d_src, d_dst = here.at[goes_up], tail_up.at[s - 1], here.at[goes_down], tail_down.at[s - 1]
        u = push(u_src, u_dst, s3.at[2 * s - 2], r3.at[2 * s - 2], up3)
        d = push(d_src, d_dst, s3.at[2 * s - 1], r3.at[2 * s - 1], down3)
        sent += [u, d]
        into_up, into_down = lax.rem(z + ahead - 1, NZ), lax.rem(z + NZ - ahead + 1, NZ)
        u.wait_recv()
        if s == 1:
            here[into_up, : rows // 2] += tail_up[0, : rows // 2]
        else:
            here[into_up] += tail_up[s - 1]
        d.wait_recv()
        if s == 1:
            here[into_down, rows // 2 :] += tail_down[0, rows // 2 :]
        else:
            here[into_down] += tail_down[s - 1]

    out[c, y] = here[z]
    done = out.at[c, y]
    copies = [push(here.at[z], done, s4.at[0], r4.at[0], partner)]
    spread = [push(here.at[z], done, s4.at[d], r4.at[d], peer) for d, peer in enumerate(ys, 1)]
    sent += copies + spread
    loss_sum(rounds, 10, NZ)
    loss_out[...] = sums[...]
    for d, copy in enumerate(spread, 1):
        copy.wait_recv()
        ref = out.at[c, lax.rem(y + NY - d, NY)]
        copies.append(push(ref, ref, s5.at[d - 1], r5.at[d - 1], partner))
        sent.append(copies[-1])
    for copy in copies:
        copy.wait_recv()
    for copy in sent:
        copy.wait_send()


def reduce_rows(grads, loss):
    total, rows, features = grads.shape
    sub = rows // (2 * NY)
    dma = pltpu.SemaphoreType.DMA
    f32 = jnp.float32
    out, loss = pl.pallas_call(
        reduce_kernel,
        in_specs=[pl.BlockSpec(memory_space=pl.ANY), pl.BlockSpec(memory_space=pltpu.VMEM)],
        out_specs=[pl.BlockSpec(memory_space=pltpu.VMEM)] * 2,
        out_shape=(jax.ShapeDtypeStruct((2, NY, sub, features), f32), jax.ShapeDtypeStruct(loss.shape, f32)),
        scratch_shapes=[
            pltpu.VMEM((4, 4, NZ, sub, features), f32),
            pltpu.VMEM((4, 4, NZ, sub, features), f32),
            pltpu.VMEM((2, NZ, sub, features), f32),
            pltpu.VMEM((2, NZ, sub, features), f32),
            pltpu.VMEM((4, NZ, sub, features), f32),
            pltpu.VMEM((4, NZ, sub, features), f32),
            pltpu.VMEM((NZ // 2, sub, features), f32),
            pltpu.VMEM((NZ // 2, sub, features), f32),
            pltpu.VMEM((NZ, sub, features), f32),
            pltpu.VMEM((NZ, sub, features), f32),
            pltpu.VMEM((NZ // 2, sub, features), f32),
            pltpu.VMEM((NZ // 2, sub, features), f32),
            pltpu.VMEM((2 + NY + NX + NZ,) + loss.shape, f32),
            pltpu.VMEM(loss.shape, f32),
            dma((16,)), dma((16,)), dma((16,)),
            dma((6,)), dma((6,)), dma((6,)), dma((6,)), dma((8,)), dma((8,)),
            dma((4,)), dma((4,)), dma((3,)), dma((3,)), dma((14,)), dma((14,)),
        ],
        compiler_params=pltpu.CompilerParams(collective_id=1, has_side_effects=True, vmem_limit_bytes=48 << 20),
        name="reduce",
    )(grads.reshape(NX, NZ, 2, NY, sub, features), loss)
    return out.reshape(rows, features), loss[0, 0]


def per_device(hidden, target, pool_table, pool_items, labels, chosen, offsets):
    user_count = lax.axis_size("users")
    length, features = hidden.shape[1:]
    factor = 1.0 / (user_count * (offsets.shape[1] - 1))
    table, items = gather(pool_table, pool_items)
    place = (lax.axis_index("seq") * length).reshape(1)
    grad_hidden, loss, grads = score(
        hidden[0], target[0], labels[0], chosen[0], offsets[0], place, table, items, factor
    )
    grad_table, loss_total = reduce_rows(grads, loss)
    return (loss_total * factor, grad_hidden[None], grad_table)


def solution(mesh):
    return jax.shard_map(
        per_device,
        mesh=mesh,
        in_specs=(
            P("users", "seq", None),
            P("users", "seq", None),
            P("users", None),
            P("users"),
            P("users", "seq"),
            P("users", "seq", None),
            P("users", None),
        ),
        out_specs=(P(), P("users", "seq", None), P("users", None)),
        check_vma=False,
    )
```

time: 616 us -> 166 us (0.27)
  waiting for transfers between devices: 301 us -> 0 us
  Pallas kernels: 0 us -> 157 us
  blocking collectives: 117 us -> 0 us
  other arithmetic: 89.1 us -> 0 us
  local copies, waits for them, and re-layouts: 50.1 us -> 6.9 us
  matrix products: 39.5 us -> 0 us
  between operations: 16.2 us -> 2.46 us
    reduce_scatter x1 -> x0, waiting for transfers between devices: 240 us -> none  [per_device(): lax.psum_scatter(grad_full, 'users', scatter_dimension=0, tiled=True)]
    pallas_call x0 -> x3, Pallas kernels: none -> 157 us  [the longest x1 79.7 us: reduce_rows(): pl.pallas_call(reduce_kernel, in_specs=[pl.BlockSpec(memory_space=pl.ANY)...]
    psum x1 -> x0, blocking collectives: 79.2 us -> none  [per_device(): loss_total = lax.psum(loss_part, ('seq', 'users')) * factor]
    scatter-add x2 -> x0, other arithmetic: 72.4 us -> none  [advance(): grad_acc.at[picked_now.reshape(-1)]]
    all_gather x1 -> x0, waiting for transfers between devices: 59.8 us -> none  [per_device(): lax.all_gather(pool_table, 'users', axis=0, tiled=True)]
    dot_general x6 -> x0, matrix products: 39.5 us -> none  [the longest x2 20.9 us: block_terms(): pool_grad = jnp.dot(neg_grad.T, narrow, preferred_element_type=jnp.float32)]
    all_gather x1 -> x0, blocking collectives: 38.2 us -> none  [per_device(): lax.all_gather(pool_items, 'users', axis=0, tiled=True)]
    gather x16 -> x0, local copies, waits for them, and re-layouts: 26.1 us -> none  [the longest x2 16.7 us: block_terms(): jnp.take(pool_rows, chosen, axis=0).reshape(-1, pool_rows.shape[2])]
  transfers between devices with their start and end apart: 3 -> 0, of which waited for: 2 -> 0; matrix products, arithmetic and copies ran while one was open for 1% -> 0% of each run, Pallas kernels for 0% -> 0%
where the time goes in v1:
time: 166 us
  Pallas kernels  157 us (95%)
  local copies, waits for them, and re-layouts  6.9 us (4%)
  between operations  2.46 us (1%)
    pallas_call x1, Pallas kernels, reduce_rows(): pl.pallas_call(reduce_kernel, in_specs=[pl.BlockSpec(memory_space=pl.ANY)...  79.7 us
    pallas_call x1, Pallas kernels, gather(): pl.pallas_call(gather_kernel, in_specs=[pl.BlockSpec(memory_space=pltpu.V...  48.3 us
    pallas_call x1, Pallas kernels, score(): pl.pallas_call(functools.partial(score_kernel, factor=factor), grid_spec=...  29.1 us
    unnamed x13, local copies, waits for them, and re-layouts  6.39 us

profile of v1, /device:TPU:1, one launch (start us, length us, event | category | flops | bytes accessed | tf_op | source)
XLA Modules:
  0.0 166.5 jit_solution(18122191065401880525)
XLA Ops:
  0.6 48.3 %gather.1 = (bf16[32,2,128,512]{3,2,1,0:T(8,128)(2,1)}, s32[32,1,256]{2,1,0:T(1,128)}) custom-call(bf16[2,128,512]{2,1,0:T(8,128)(2,1)} %bitcast.21, s32[1,256]{1,0:T(1,128)} %bitcast.22), custom_call_target="tpu_custom_call" | custom-call | tf_op jit(solution)/shard_map/gather/pallas_call | solution.py:135
  49.0 0.0 copy-start
  49.0 1.6 copy-done
  50.6 0.0 copy-start.1
  50.6 1.2 copy-done.1
  51.8 0.0 copy-start.2
  51.8 0.8 copy-done.2
  52.5 0.0 copy-start.3
  52.5 0.7 copy-done.3
  53.2 0.0 copy-start.4
  53.2 0.7 copy-done.4
  53.9 0.0 copy-start.5
  53.9 0.7 copy-done.5
  54.6 29.1 %score.1 = (f32[1024,512]{1,0:T(8,128)}, f32[8,128]{1,0:T(8,128)S(1)}, f32[32,256,512]{2,1,0:T(8,128)}) custom-call(s32[8,8]{1,0:T(8,128)S(1)} %bitcast.16, s32[5]{0:T(128)S(1)} %bitcast.18, s32[1]{0:T(128)} %bitcast.2.place_s, f32[1024,512]{1,0:T(8,128)S(1)} %bitcast.13, bf16[1024,512]{1,0:T(8,128)(2,1)S(1)} %bitcast.14, s32[8,1,128]{2,1,0:T(1,128)S(1)} %bitcast.17, ...), custom_call_target="tpu_custom_call" | custom-call | tf_op jit(solution)/shard_map/score/pallas_call | solution.py:262
  83.7 79.7 %reduce.1 = (f32[2,4,32,512]{3,2,1,0:T(8,128)S(1)}, f32[8,128]{1,0:T(8,128)S(1)}) custom-call(f32[4,8,2,4,32,512]{5,4,3,2,1,0:T(8,128)} %bitcast.19, f32[8,128]{1,0:T(8,128)S(1)} %get-tuple-element.13.loss_in), custom_call_target="tpu_custom_call" | custom-call | tf_op jit(solution)/shard_map/reduce/pallas_call | solution.py:462
  163.4 0.5 slice.3
  164.5 0.8 copy.11
Async XLA Ops:
  49.0 1.6 copy-start
  50.6 1.2 copy-start.1
  51.8 0.8 copy-start.2
  52.5 0.7 copy-start.3
  53.2 0.7 copy-start.4
  53.9 0.7 copy-start.5

commit v2 on v1

v2 whole, which is shorter than its diff:
```python
import functools
import jax
import jax.numpy as jnp
from jax import lax
from jax.experimental import pallas as pl
from jax.experimental.pallas import tpu as pltpu
from jax.sharding import PartitionSpec as P

MESH = pl.DeviceIdType.MESH
NX, NY, NZ = 4, 4, 8


def where_am_i():
    seq, users = lax.axis_index("seq"), lax.axis_index("users")
    return users // NZ, seq // 2, users % NZ, seq % 2


def device(x, y, z, c):
    return {"seq": y * 2 + c, "users": x * NZ + z}


def greet(peers):
    barrier = pltpu.get_barrier_semaphore()
    for peer in peers:
        pl.semaphore_signal(barrier, inc=1, device_id=peer, device_id_type=MESH)
    pl.semaphore_wait(barrier, len(peers))


def push(src, dst, send_sem, recv_sem, to):
    copy = pltpu.make_async_remote_copy(src_ref=src, dst_ref=dst, send_sem=send_sem, recv_sem=recv_sem,
                                        device_id=to, device_id_type=MESH)
    copy.start()
    return copy


def gather_kernel(shard, items, chosen, table, all_items, both, local_sem, pair_sem, partner_send, partner_recv,
                  item_send, item_recv, send1, recv1, send2, recv2):
    x, y, z, c = where_am_i()
    users = x * NZ + z
    total = NX * NZ
    quarter = shard.shape[1] // 2
    others = [lax.rem(users + d, total) for d in range(1, total)]
    partner = device(x, y, z, 1 - c)
    greet([{"seq": y * 2 + c, "users": u} for u in others] + [partner])

    mine = pltpu.make_async_copy(shard, table.at[users], local_sem.at[0])
    mine.start()
    mine_items = pltpu.make_async_copy(items, all_items.at[users], local_sem.at[1])
    mine_items.start()
    mine_chosen = pltpu.make_async_copy(chosen, both.at[c], local_sem.at[2])
    mine_chosen.start()
    theirs = push(chosen, both.at[c], pair_sem.at[0], pair_sem.at[1], partner)

    def run(n1, n2, me1, me2, region, dev):
        copies, pending = [], {}

        def part(ref, s, n, d):
            return ref if s < n // 2 else ref.at[pl.ds(0 if d > 0 else quarter, quarter)]

        def size(ring):
            return n1 if ring == 1 else n2

        def place(ring, sub, back):
            if ring == 1:
                return lax.rem(me1 - back + n1, n1), me2
            return lax.rem(me1 + sub + n1, n1), lax.rem(me2 - back + n2, n2)

        def send(ring, sub, s, d):
            n = size(ring)
            dst = region(*place(ring, sub, d * (s - 1)))
            src = shard.at[c] if s == 1 and sub == 0 else dst
            if ring == 1:
                k = (s - 1) * 2 + (d < 0)
                sems, to = (send1.at[k], recv1.at[k]), dev(lax.rem(me1 + d + n, n), me2)
            else:
                k = ((sub % n1) * (n2 // 2) + s - 1) * 2 + (d < 0)
                sems, to = (send2.at[k], recv2.at[k]), dev(me1, lax.rem(me2 + d + n, n))
            copy = push(part(src, s, n, d), part(dst, s, n, d), *sems, to)
            copies.append(copy)
            pending[ring, sub, s, d] = copy

        passed = []

        def arrive(ring, sub, s, d):
            pending.pop((ring, sub, s, d)).wait_recv()
            ref = part(region(*place(ring, sub, d * s)), s, size(ring), d)
            passed.append(push(ref, ref, partner_send.at[len(passed)], partner_recv, partner))

        ready = {0: 0}
        for s in range(1, n1 // 2):
            ready[-s], ready[s] = s, s
        ready[n1 // 2] = n1 // 2
        for time in range(1, n1 // 2 + n2 // 2 + 2):
            if time <= n1 // 2 + 1:
                for d in (1, -1):
                    if time > 1:
                        arrive(1, 0, time - 1, d)
                    if time <= n1 // 2:
                        send(1, 0, time, d)
            for sub, at in ready.items():
                s = time - at
                if 1 <= s <= n2 // 2 + 1:
                    for d in (1, -1):
                        if s > 1:
                            arrive(2, sub, s - 1, d)
                        if s <= n2 // 2:
                            send(2, sub, s, d)
        assert not pending
        for copy in copies + passed:
            copy.wait_send()

    shared = [push(items, all_items.at[users], item_send.at[d], item_recv, {"seq": y * 2 + c, "users": u})
              for d, u in enumerate(others)]

    @pl.when(c == 0)
    def _():
        run(NX, NZ, x, z, lambda i1, i2: table.at[i1 * NZ + i2, 0], lambda i1, i2: device(i1, y, i2, 0))

    @pl.when(c == 1)
    def _():
        run(NZ, NX, z, x, lambda i1, i2: table.at[i2 * NZ + i1, 1], lambda i1, i2: device(i2, y, i1, 1))

    for copy in shared:
        copy.wait_send()
    rest = all_items.at[pl.ds(0, total - 1)]
    pltpu.make_async_copy(rest, rest, item_recv).wait()
    rest = table.at[pl.ds(0, total - 1), 0]
    pltpu.make_async_copy(rest, rest, partner_recv).wait()
    mine.wait()
    mine_items.wait()
    mine_chosen.wait()
    theirs.wait()


def gather(pool_table, pool_items, chosen):
    rows, features = pool_table.shape
    total = NX * NZ
    dma = pltpu.SemaphoreType.DMA
    anywhere = pl.BlockSpec(memory_space=pl.ANY)
    table, items, both = pl.pallas_call(
        gather_kernel,
        in_specs=[pl.BlockSpec(memory_space=pltpu.VMEM)] * 3,
        out_specs=[anywhere] * 3,
        out_shape=(
            jax.ShapeDtypeStruct((total, 2, rows // 2, features), pool_table.dtype),
            jax.ShapeDtypeStruct((total, 1, rows), pool_items.dtype),
            jax.ShapeDtypeStruct((2,) + chosen.shape, chosen.dtype),
        ),
        scratch_shapes=[dma((3,)), dma((2,)), dma((40,)), dma, dma((total - 1,)), dma, dma((8,)), dma((8,)), dma((32,)),
                        dma((32,))],
        compiler_params=pltpu.CompilerParams(collective_id=0, has_side_effects=True),
        name="gather",
    )(pool_table.reshape(2, rows // 2, features), pool_items.reshape(1, rows), chosen)
    return table.reshape(total, rows, features), items, both


NB = 256
PB = 128


def score_kernel(chosen_s, offsets_s, place_s, hidden_ref, target_ref, labels_ref, table_ref, items_ref,
                 gh_ref, loss_ref, shares_ref, narrow_ref, slots_ref, scores, loss_acc, *, factor):
    b = pl.program_id(0)
    blocks = pl.num_programs(0)
    pair, _, kb = chosen_s.shape
    count = table_ref.shape[0]
    hists = offsets_s.shape[0] - 1
    core = place_s[1]
    base = place_s[0] + b * PB

    for other in range(pair):
        for k in range(count):
            slots_ref[other * blocks + b, k] = kb
    for other in range(pair):
        for j in range(kb):
            slots_ref[other * blocks + b, chosen_s[other, b, j]] = j

    @pl.when(b == 0)
    def _():
        loss_acc[...] = jnp.zeros_like(loss_acc)

    live = base < offsets_s[hists]
    narrow = hidden_ref[...].astype(jnp.bfloat16)
    narrow_ref[...] = narrow

    @pl.when(jnp.logical_not(live))
    def _():
        gh_ref[...] = jnp.zeros_like(gh_ref)
        shares_ref[...] = jnp.zeros_like(shares_ref)

    @pl.when(live)
    def _():
        target_wide = target_ref[...].astype(jnp.float32)
        positive = jnp.sum(narrow.astype(jnp.float32) * target_wide, axis=1, keepdims=True)
        labels = jnp.broadcast_to(labels_ref[0], (PB, PB)).T[:, :1]
        positions = base + lax.broadcasted_iota(jnp.int32, (PB, 1), 0)
        weights = jnp.zeros((PB, 1), jnp.float32)
        for h in range(hists):
            start, finish = offsets_s[h], offsets_s[h + 1]
            length = jnp.broadcast_to(finish - start, (PB, 1)).astype(jnp.float32)
            inside = (positions >= start) & (positions < finish)
            weights = weights + jnp.where(inside, 1.0 / length, 0.0)

        top = jnp.full((PB, 128), -1e30, jnp.float32)
        for j in range(kb):
            k = chosen_s[core, b, j]
            raw = lax.dot_general(narrow, table_ref[k], (((1,), (1,)), ((), ())),
                                  preferred_element_type=jnp.float32)
            masked = jnp.where(items_ref[k] == labels, -1e30, raw)
            scores[:, j * NB:(j + 1) * NB] = masked
            for i in range(NB // 128):
                top = jnp.maximum(top, masked[:, i * 128:(i + 1) * 128])
        peak = jnp.maximum(positive, jnp.max(top, axis=1, keepdims=True))
        added = jnp.zeros((PB, 128), jnp.float32)
        for j in range(kb):
            each = jnp.exp(scores[:, j * NB:(j + 1) * NB] - peak)
            scores[:, j * NB:(j + 1) * NB] = each
            for i in range(NB // 128):
                added = added + each[:, i * 128:(i + 1) * 128]
        pos_exp = jnp.exp(positive - peak)
        totals = pos_exp + jnp.sum(added, axis=1, keepdims=True)
        cross = peak + jnp.log(totals) - positive
        loss_acc[...] += jnp.broadcast_to(jnp.sum(weights * cross, axis=0, keepdims=True), loss_acc.shape)
        coeff = weights * factor
        scale = coeff / totals
        pos_grad = coeff * (pos_exp / totals - 1.0)
        out = pos_grad * target_wide
        for j in range(kb):
            k = chosen_s[core, b, j]
            g = (scores[:, j * NB:(j + 1) * NB] * scale).astype(jnp.bfloat16)
            gt = g.T
            shares_ref[0, 0, j] = gt[:128]
            shares_ref[1, 0, j] = gt[128:]
            out = out + jnp.dot(g, table_ref[k], preferred_element_type=jnp.float32)
        gh_ref[...] = out

    @pl.when(b == blocks - 1)
    def _():
        loss_ref[...] = loss_acc[...]


def score(hidden, target, labels, chosen, offsets, place, table, items, factor):
    rows, features = hidden.shape
    blocks = rows // PB
    count = table.shape[0]
    pair, _, kb = chosen.shape
    half = NB // 2
    one = pl.Buffered(1)
    grid_spec = pltpu.PrefetchScalarGridSpec(
        num_scalar_prefetch=3,
        grid=(blocks,),
        in_specs=[
            pl.BlockSpec((PB, features), lambda b, *_: (b, 0)),
            pl.BlockSpec((PB, features), lambda b, *_: (b, 0)),
            pl.BlockSpec((1, 1, PB), lambda b, *_: (b, 0, 0)),
            pl.BlockSpec((count, NB, features), lambda b, *_: (0, 0, 0), pipeline_mode=one),
            pl.BlockSpec((count, 1, NB), lambda b, *_: (0, 0, 0), pipeline_mode=one),
        ],
        out_specs=[
            pl.BlockSpec((PB, features), lambda b, *_: (b, 0)),
            pl.BlockSpec((8, 128), lambda b, *_: (0, 0)),
            pl.BlockSpec((2, 1, kb, half, PB), lambda b, *_: (0, b, 0, 0, 0)),
            pl.BlockSpec((PB, features), lambda b, *_: (b, 0)),
            pl.BlockSpec(memory_space=pltpu.SMEM),
        ],
        scratch_shapes=[
            pltpu.VMEM((PB, kb * NB), jnp.float32),
            pltpu.VMEM((8, 128), jnp.float32),
        ],
    )
    return pl.pallas_call(
        functools.partial(score_kernel, factor=factor),
        grid_spec=grid_spec,
        out_shape=(
            jax.ShapeDtypeStruct((rows, features), jnp.float32),
            jax.ShapeDtypeStruct((8, 128), jnp.float32),
            jax.ShapeDtypeStruct((2, blocks, kb, half, PB), jnp.bfloat16),
            jax.ShapeDtypeStruct((rows, features), jnp.bfloat16),
            jax.ShapeDtypeStruct((pair * blocks, count), jnp.int32),
        ),
        compiler_params=pltpu.CompilerParams(vmem_limit_bytes=60 << 20),
        name="score",
    )(chosen, offsets, place, hidden, target, labels.reshape(blocks, 1, PB), table, items)


def reduce_kernel(shares, narrow, slots, loss_in, out, loss_out, lists, wide, own, landing, landing2, landing3, parts,
                  sums, load_sem, pair_send, pair_recv, s1, r1, s2, r2, s3, r3, s4, r4, s5, r5, loss_send, loss_recv):
    x, y, z, c = where_am_i()
    partner = device(x, y, z, 1 - c)
    xs = [device(lax.rem(x + d, NX), y, z, c) for d in range(1, NX)]
    ys = [device(x, lax.rem(y + d, NY), z, c) for d in range(1, NY)]
    zs = [device(x, y, lax.rem(z + d, NZ), c) for d in range(1, NZ)]
    blocks, kb = shares.shape[1:3]
    rows = own.shape[1]
    sub = rows // NY
    length = narrow.shape[0]

    greet([partner] + xs + ys + zs)
    sent = [
        push(shares.at[1 - c], lists.at[pl.ds(c * blocks, blocks), pl.ds(0, kb)], pair_send.at[0], pair_recv.at[0], partner),
        push(narrow, wide.at[pl.ds(c * length, length)], pair_send.at[1], pair_recv.at[1], partner),
    ]
    loads = [
        pltpu.make_async_copy(shares.at[c], lists.at[pl.ds(c * blocks, blocks), pl.ds(0, kb)], load_sem.at[0]),
        pltpu.make_async_copy(narrow, wide.at[pl.ds(c * length, length)], load_sem.at[1]),
    ]
    for copy in loads:
        copy.start()
    for i in range(2 * blocks):
        lists[i, kb] = jnp.zeros(lists.shape[2:], lists.dtype)

    def loss_round(k, base, me, peers):
        parts[base + me] = sums[...]
        return [push(sums, parts.at[base + me], loss_send.at[k + d], loss_recv.at[k + d], peer)
                for d, peer in enumerate(peers)]

    def loss_sum(copies, base, count):
        for copy in copies:
            copy.wait()
        total = parts[base]
        for i in range(1, count):
            total = total + parts[base + i]
        sums[...] = total

    sums[...] = loss_in[...]
    loss_sum(loss_round(0, 0, c, [partner]), 0, 2)
    copies = loss_round(1, 2, y, ys)
    for copy in loads + sent:
        copy.wait()
    loss_sum(copies, 2, NY)
    copies = loss_round(4, 6, x, xs)

    def half(ref, h):
        size = ref.shape[0] // 2
        return ref.at[pl.ds(h * size, size)]

    def add(dst, src):
        step = 16

        @pl.loop(0, dst.shape[0] // step)
        def _(i):
            here = pl.ds(pl.multiple_of(i * step, step), step)
            dst[here] += src[here]

    def tree(n, me, subs, chunk, land, send_sems, recv_sems, up, down, before=None):
        old = {}
        for s in range(1, n // 2 + 2):
            ahead = n // 2 + 1 - s
            if before is not None:
                before(ahead)
            for j in range(subs):
                for d, to in ((1, up), (-1, down)):
                    ref = chunk(lax.rem(me + d * ahead + n, n), j)
                    if s > 1:
                        slot = ((s - 2) * subs + j) * 2 + (d < 0)
                        old[slot].wait_recv()
                        if s == 2:
                            add(half(ref, d < 0), half(land.at[slot], d < 0))
                        else:
                            add(ref, land.at[slot])
                    if ahead:
                        slot = ((s - 1) * subs + j) * 2 + (d < 0)
                        dst = land.at[slot]
                        if s == 1:
                            ref, dst = half(ref, d < 0), half(dst, d < 0)
                        old[slot] = push(ref, dst, send_sems.at[slot], recv_sems.at[slot], to)
        return list(old.values())

    group = 4

    def produce(first, count, block):
        @pl.loop(0, count)
        def _(g):
            base = (first + g) * group
            lhs = []
            for i in range(group):
                k = block(base + i)
                lhs.append(jnp.concatenate([lists[b, slots[b, k]] for b in range(2 * blocks)], axis=1))
            total = jnp.dot(jnp.concatenate(lhs, axis=0), wide[...], preferred_element_type=jnp.float32)
            for i in range(group):
                own[base + i] = total[i * rows:(i + 1) * rows]

    def run(n1, n2, me1, me2, dev, block):
        def chunk(i1, j):
            return own.at[i1 * n2 + j]

        per = n2 // group

        def before(ahead):
            if ahead == 0 or ahead == n1 // 2:
                produce(lax.rem(me1 + ahead, n1) * per, per, block)
            else:
                for d in (1, -1):
                    produce(lax.rem(me1 + d * ahead + n1, n1) * per, per, block)

        sent = tree(n1, me1, n2, chunk, landing, s1, r1, dev(lax.rem(me1 + 1, n1), me2),
                    dev(lax.rem(me1 + n1 - 1, n1), me2), before)

        def piece(i2, j):
            return own.at[me1 * n2 + i2, pl.ds(j * sub, sub)]

        sent += tree(n2, me2, NY, piece, landing2, s2, r2, dev(me1, lax.rem(me2 + 1, n2)),
                     dev(me1, lax.rem(me2 + n2 - 1, n2)))
        for copy in sent:
            copy.wait_send()

    @pl.when(c == 0)
    def _():
        run(NZ, NX, z, x, lambda i1, i2: device(i2, y, i1, 0), lambda t: (t % NX) * NZ + t // NX)

    @pl.when(c == 1)
    def _():
        run(NX, NZ, x, z, lambda i1, i2: device(i1, y, i2, 1), lambda t: t)

    loss_sum(copies, 6, NX)
    copies = loss_round(7, 10, z, zs)
    mine = own.at[(z * NX + x) * (1 - c) + (x * NZ + z) * c]
    sent = tree(NY, y, 1, lambda i, j: mine.at[pl.ds(i * sub, sub)], landing3, s3, r3, ys[0], ys[-1])

    ready = mine.at[pl.ds(y * sub, sub)]
    out[c, y] = ready[...]
    done = out.at[c, y]
    swaps = [push(ready, done, s4.at[0], r4.at[0], partner)]
    spread = [push(ready, done, s4.at[d], r4.at[d], peer) for d, peer in enumerate(ys, 1)]
    loss_sum(copies, 10, NZ)
    loss_out[...] = sums[...]
    for d, copy in enumerate(spread, 1):
        copy.wait_recv()
        ref = out.at[c, lax.rem(y + NY - d, NY)]
        swaps.append(push(ref, ref, s5.at[d - 1], r5.at[d - 1], partner))
    for copy in swaps:
        copy.wait_recv()
    for copy in sent + spread + swaps:
        copy.wait_send()


def reduce_rows(shares, narrow, slots, loss):
    pair, blocks, kb, half, width = shares.shape
    length, features = narrow.shape
    total = NX * NZ
    sub = half // NY
    dma = pltpu.SemaphoreType.DMA
    f32 = jnp.float32
    anywhere = pl.BlockSpec(memory_space=pl.ANY)
    vmem = pl.BlockSpec(memory_space=pltpu.VMEM)
    out, loss = pl.pallas_call(
        reduce_kernel,
        in_specs=[anywhere, anywhere, pl.BlockSpec(memory_space=pltpu.SMEM), vmem],
        out_specs=[vmem, vmem],
        out_shape=(jax.ShapeDtypeStruct((2, NY, sub, features), f32), jax.ShapeDtypeStruct(loss.shape, f32)),
        scratch_shapes=[
            pltpu.VMEM((pair * blocks, kb + 1, half, width), shares.dtype),
            pltpu.VMEM((pair * length, features), narrow.dtype),
            pltpu.VMEM((total, half, features), f32),
            pltpu.VMEM((32, half, features), f32),
            pltpu.VMEM((32, sub, features), f32),
            pltpu.VMEM((4, sub, features), f32),
            pltpu.VMEM((2 + NY + NX + NZ,) + loss.shape, f32),
            pltpu.VMEM(loss.shape, f32),
            dma((2,)), dma((2,)), dma((2,)),
            dma((32,)), dma((32,)), dma((32,)), dma((32,)), dma((4,)), dma((4,)),
            dma((4,)), dma((4,)), dma((3,)), dma((3,)), dma((14,)), dma((14,)),
        ],
        compiler_params=pltpu.CompilerParams(collective_id=1, has_side_effects=True, vmem_limit_bytes=56 << 20),
        name="reduce",
    )(shares, narrow, slots, loss)
    return out.reshape(2 * half, features), loss[0, 0]


def per_device(hidden, target, pool_table, pool_items, labels, chosen, offsets):
    user_count = lax.axis_size("users")
    length, features = hidden.shape[1:]
    factor = 1.0 / (user_count * (offsets.shape[1] - 1))
    table, items, both = gather(pool_table, pool_items, chosen[0])
    seq = lax.axis_index("seq")
    place = jnp.stack([seq * length, seq % 2])
    grad_hidden, loss, shares, narrow, slots = score(
        hidden[0], target[0], labels[0], both, offsets[0], place, table, items, factor
    )
    grad_table, loss_total = reduce_rows(shares, narrow, slots, loss)
    return (loss_total * factor, grad_hidden[None], grad_table)


def solution(mesh):
    return jax.shard_map(
        per_device,
        mesh=mesh,
        in_specs=(
            P("users", "seq", None),
            P("users", "seq", None),
            P("users", None),
            P("users"),
            P("users", "seq"),
            P("users", "seq", None),
            P("users", None),
        ),
        out_specs=(P(), P("users", "seq", None), P("users", None)),
        check_vma=False,
    )
```

time: 166 us -> 160 us (0.964)
  local copies, waits for them, and re-layouts: 6.9 us -> 3.06 us
  Pallas kernels: 157 us -> 154 us
    pallas_call x1, Pallas kernels: 29.1 us -> 18.8 us  [score(): pl.pallas_call(functools.partial(score_kernel, factor=factor), grid_spec=...]
    pallas_call x1, Pallas kernels: 79.7 us -> 86.5 us  [reduce_rows(): pl.pallas_call(reduce_kernel, in_specs=[anywhere, anywhere, pl.BlockSpec(...]
    unnamed x13 -> x1, local copies, waits for them, and re-layouts: 6.39 us -> 1.87 us
where the time goes in v2:
time: 160 us
  Pallas kernels  154 us (96%)
  local copies, waits for them, and re-layouts  3.06 us (2%)
  between operations  2.44 us (2%)
    pallas_call x1, Pallas kernels, reduce_rows(): pl.pallas_call(reduce_kernel, in_specs=[anywhere, anywhere, pl.BlockSpec(...  86.5 us
    pallas_call x1, Pallas kernels, gather(): pl.pallas_call(gather_kernel, in_specs=[pl.BlockSpec(memory_space=pltpu.V...  48.3 us
    pallas_call x1, Pallas kernels, score(): pl.pallas_call(functools.partial(score_kernel, factor=factor), grid_spec=...  18.8 us

profile of v2, /device:TPU:1, one launch (start us, length us, event | category | flops | bytes accessed | tf_op | source)
XLA Modules:
  0.0 159.6 jit_solution(6806298565561835954)
XLA Ops:
  0.6 0.6 pad_add_fusion.place_s
  1.2 48.3 %gather.1 = (bf16[32,2,128,512]{3,2,1,0:T(8,128)(2,1)}, s32[32,1,256]{2,1,0:T(1,128)}, s32[2,8,8]{2,1,0:T(8,128)}) custom-call(bf16[2,128,512]{2,1,0:T(8,128)(2,1)} %bitcast.17, s32[1,256]{1,0:T(1,128)} %bitcast.20, s32[8,8]{1,0:T(8,128)} %bitcast.19), custom_call_target="tpu_custom_call" | custom-call | tf_op jit(solution)/shard_map/gather/pallas_call | solution.py:140
  49.5 18.8 %score.1 = (f32[1024,512]{1,0:T(8,128)}, f32[8,128]{1,0:T(8,128)}, bf16[2,8,8,128,128]{4,3,2,1,0:T(8,128)(2,1)}, bf16[1024,512]{1,0:T(8,128)(2,1)}, s32[16,32]{1,0:T(8,128)}) custom-call(s32[2,8,8]{2,1,0:T(8,128)} %get-tuple-element.13.chosen_s, s32[5]{0:T(128)} %bitcast.21, s32[2]{0:T(128)} %pad_add_fusion.place_s, f32[1024,512]{1,0:T(8,128)} %bitcast.14, ...), custom_call_target="tpu_custom_call" | custom-call | tf_op jit(solution)/shard_map/score/pallas_call | solution.py:271
  68.3 86.5 %reduce.1 = (f32[2,4,32,512]{3,2,1,0:T(8,128)}, f32[8,128]{1,0:T(8,128)}) custom-call(bf16[2,8,8,128,128]{4,3,2,1,0:T(8,128)(2,1)} %get-tuple-element.16.shares, bf16[1024,512]{1,0:T(8,128)(2,1)} %get-tuple-element.17.narrow, s32[16,32]{1,0:T(8,128)} %get-tuple-element.18.slots, f32[8,128]{1,0:T(8,128)} %get-tuple-element.19.loss_in), custom_call_target="tpu_custom_call" | custom-call | tf_op jit(solution)/shard_map/reduce/pallas_call | solution.py:446
  154.8 1.2 slice.3
  156.6 1.9 %copy.11 = f32[256,512]{1,0:T(8,128)} copy(f32[256,512]{1,0:T(8,128)} %bitcast.16) | data formatting | bytes 1048576

commit v3 on v2

v3 whole, which is shorter than its diff:
```python
import functools
import jax
import jax.numpy as jnp
from jax import lax
from jax.experimental import pallas as pl
from jax.experimental.pallas import tpu as pltpu
from jax.sharding import PartitionSpec as P

MESH = pl.DeviceIdType.MESH
NX, NY, NZ = 4, 4, 8
EXTRA = 16


def where_am_i():
    seq, users = lax.axis_index("seq"), lax.axis_index("users")
    return users // NZ, seq // 2, users % NZ, seq % 2


def device(x, y, z, c):
    return {"seq": y * 2 + c, "users": x * NZ + z}


def greet(peers):
    barrier = pltpu.get_barrier_semaphore()
    for peer in peers:
        pl.semaphore_signal(barrier, inc=1, device_id=peer, device_id_type=MESH)
    pl.semaphore_wait(barrier, len(peers))


def push(src, dst, send_sem, recv_sem, to):
    copy = pltpu.make_async_remote_copy(src_ref=src, dst_ref=dst, send_sem=send_sem, recv_sem=recv_sem,
                                        device_id=to, device_id_type=MESH)
    copy.start()
    return copy


def gather_kernel(shard, items, chosen, table, both, whole, local_sem, pair_sem, partner_send, partner_recv, send1, recv1, send2, recv2):
    x, y, z, c = where_am_i()
    users = x * NZ + z
    total = NX * NZ
    rows = shard.shape[0]
    cut = rows * 3 // 8
    partner = device(x, y, z, 1 - c)

    whole[:rows] = shard[...]
    high = items[...] // 128
    digits = jnp.concatenate([high, items[...] - high * 128], axis=1).astype(jnp.float32)
    whole[rows:] = jnp.broadcast_to(digits, (EXTRA, digits.shape[1])).astype(whole.dtype)
    rows = rows + EXTRA

    greet([partner] + [device(lax.rem(x + d, NX), y, z, c) for d in range(1, NX)]
          + [device(x, y, lax.rem(z + d, NZ), c) for d in (1, 2, NZ - 2, NZ - 1)])
    mine = pltpu.make_async_copy(whole, table.at[users], local_sem.at[0])
    mine.start()
    mine_chosen = pltpu.make_async_copy(chosen, both.at[c], local_sem.at[1])
    mine_chosen.start()
    theirs = push(chosen, both.at[c], pair_sem.at[0], pair_sem.at[1], partner)

    def run(plan, n1, n2, me1, me2, start, count, where, dev):
        copies, pending = [], {}
        quarter = count // 2

        def region(i1, i2):
            return table.at[where(i1, i2), pl.ds(start, count)]

        def part(ref, h):
            return ref if h is None else ref.at[pl.ds(h * quarter, quarter)]

        def at(rel1, rel2):
            return region(lax.rem(me1 + rel1 + n1, n1), lax.rem(me2 + rel2 + n2, n2))

        def send(key, rel1, rel2, h, sems, to):
            dst = part(at(rel1, rel2), h)
            src = part(whole.at[pl.ds(start, count)], h) if rel1 == 0 and rel2 == 0 else dst
            pending[key] = push(src, dst, *sems, to)
            copies.append(pending[key])

        passed = []

        def arrive(key, rel1, rel2, h):
            pending.pop(key).wait_recv()
            ref = part(at(rel1, rel2), h)
            passed.append(push(ref, ref, partner_send.at[len(passed)], partner_recv, partner))

        ready = {0: 0}
        for stage, back, ahead, h in plan:
            ready[-back - ahead if abs(back + ahead) < n1 // 2 else n1 // 2] = stage
        stages = max(ready.values())
        for time in range(1, stages + n2 // 2 + 2):
            for i, (stage, back, ahead, h) in enumerate(plan):
                if stage == time - 1:
                    arrive((1, i), -back - ahead, 0, h)
            for i, (stage, back, ahead, h) in enumerate(plan):
                if stage == time:
                    send((1, i), -back, 0, h, (send1.at[i], recv1.at[i]), dev(lax.rem(me1 + ahead + n1, n1), me2))
            for sub, when in ready.items():
                s = time - when
                for d in (1, -1):
                    if 2 <= s <= n2 // 2 + 1:
                        h = None if s - 1 < n2 // 2 else int(d < 0)
                        arrive((2, sub, s - 1, d), sub, -d * (s - 1), h)
                    if 1 <= s <= n2 // 2:
                        h = None if s < n2 // 2 else int(d < 0)
                        k = ((sub % n1) * (n2 // 2) + s - 1) * 2 + (d < 0)
                        send((2, sub, s, d), sub, -d * (s - 1), h, (send2.at[k], recv2.at[k]),
                             dev(me1, lax.rem(me2 + d + n2, n2)))
        assert not pending
        for copy in copies + passed:
            copy.wait_send()
        rest = table.at[pl.ds(0, total - 1), pl.ds(0, start) if start else pl.ds(count, rows - count)]
        pltpu.make_async_copy(rest, rest, partner_recv).wait()

    across = [(1, 0, 1, None), (1, 0, -1, None), (1, 0, 2, None)]
    along = [(1, 0, 1, None), (1, 0, -1, None), (1, 0, 2, None), (1, 0, -2, None),
             (2, 2, 1, None), (2, -2, -1, None), (2, 2, 2, 0), (2, -2, -2, 1)]

    @pl.when(c == 0)
    def _():
        run(across, NX, NZ, x, z, 0, cut, lambda i1, i2: i1 * NZ + i2, lambda i1, i2: device(i1, y, i2, 0))

    @pl.when(c == 1)
    def _():
        run(along, NZ, NX, z, x, cut, rows - cut, lambda i1, i2: i2 * NZ + i1, lambda i1, i2: device(i2, y, i1, 1))

    mine.wait()
    mine_chosen.wait()
    theirs.wait()


def gather(pool_table, pool_items, chosen):
    rows, features = pool_table.shape
    total = NX * NZ
    dma = pltpu.SemaphoreType.DMA
    anywhere = pl.BlockSpec(memory_space=pl.ANY)
    table, both = pl.pallas_call(
        gather_kernel,
        in_specs=[pl.BlockSpec(memory_space=pltpu.VMEM)] * 3,
        out_specs=[anywhere] * 2,
        out_shape=(
            jax.ShapeDtypeStruct((total, rows + EXTRA, features), pool_table.dtype),
            jax.ShapeDtypeStruct((2,) + chosen.shape, chosen.dtype),
        ),
        scratch_shapes=[pltpu.VMEM((rows + EXTRA, features), pool_table.dtype),
                        dma((2,)), dma((2,)), dma((40,)), dma, dma((8,)), dma((8,)), dma((32,)),
                        dma((32,))],
        compiler_params=pltpu.CompilerParams(collective_id=0, has_side_effects=True),
        name="gather",
    )(pool_table, pool_items.reshape(1, rows), chosen)
    return table, both


NB = 256
PB = 128


def score_kernel(chosen_s, offsets_s, hidden_ref, target_ref, labels_ref, table_ref,
                 gh_ref, loss_ref, shares_ref, narrow_ref, slots_ref, scores, loss_acc, *, factor):
    b = pl.program_id(0)
    blocks = pl.num_programs(0)
    pair, _, kb = chosen_s.shape
    count = table_ref.shape[0]
    hists = offsets_s.shape[0] - 1
    seq = lax.axis_index("seq")
    core = seq % 2
    base = (seq * blocks + b) * PB

    for other in range(pair):
        for k in range(count):
            slots_ref[other * blocks + b, k] = kb
    for other in range(pair):
        for j in range(kb):
            slots_ref[other * blocks + b, chosen_s[other, b, j]] = j

    @pl.when(b == 0)
    def _():
        loss_acc[...] = jnp.zeros_like(loss_acc)

    live = base < offsets_s[hists]
    narrow = hidden_ref[...].astype(jnp.bfloat16)
    narrow_ref[...] = narrow

    @pl.when(jnp.logical_not(live))
    def _():
        gh_ref[...] = jnp.zeros_like(gh_ref)
        shares_ref[...] = jnp.zeros_like(shares_ref)

    @pl.when(live)
    def _():
        target_wide = target_ref[...].astype(jnp.float32)
        positive = jnp.sum(narrow.astype(jnp.float32) * target_wide, axis=1, keepdims=True)
        labels = jnp.broadcast_to(labels_ref[0].astype(jnp.float32), (PB, PB)).T[:, :1]
        positions = base + lax.broadcasted_iota(jnp.int32, (PB, 1), 0)
        weights = jnp.zeros((PB, 1), jnp.float32)
        for h in range(hists):
            start, finish = offsets_s[h], offsets_s[h + 1]
            length = jnp.broadcast_to(finish - start, (PB, 1)).astype(jnp.float32)
            inside = (positions >= start) & (positions < finish)
            weights = weights + jnp.where(inside, 1.0 / length, 0.0)

        top = jnp.full((PB, 128), -1e30, jnp.float32)
        for j in range(kb):
            k = chosen_s[core, b, j]
            rows = table_ref[k, :NB]
            digits = table_ref[k, NB:][:1].astype(jnp.float32)
            items = digits[:, :NB] * 128.0 + digits[:, NB:]
            raw = lax.dot_general(narrow, rows, (((1,), (1,)), ((), ())),
                                  preferred_element_type=jnp.float32)
            masked = jnp.where(items == labels, -1e30, raw)
            scores[:, j * NB:(j + 1) * NB] = masked
            for i in range(NB // 128):
                top = jnp.maximum(top, masked[:, i * 128:(i + 1) * 128])
        peak = jnp.maximum(positive, jnp.max(top, axis=1, keepdims=True))
        added = jnp.zeros((PB, 128), jnp.float32)
        for j in range(kb):
            each = jnp.exp(scores[:, j * NB:(j + 1) * NB] - peak)
            scores[:, j * NB:(j + 1) * NB] = each
            for i in range(NB // 128):
                added = added + each[:, i * 128:(i + 1) * 128]
        pos_exp = jnp.exp(positive - peak)
        totals = pos_exp + jnp.sum(added, axis=1, keepdims=True)
        cross = peak + jnp.log(totals) - positive
        loss_acc[...] += jnp.broadcast_to(jnp.sum(weights * cross, axis=0, keepdims=True), loss_acc.shape)
        coeff = weights * factor
        scale = coeff / totals
        pos_grad = coeff * (pos_exp / totals - 1.0)
        out = pos_grad * target_wide
        for j in range(kb):
            k = chosen_s[core, b, j]
            g = (scores[:, j * NB:(j + 1) * NB] * scale).astype(jnp.bfloat16)
            gt = g.T
            shares_ref[0, 0, j] = gt[:128]
            shares_ref[1, 0, j] = gt[128:]
            out = out + jnp.dot(g, table_ref[k, :NB], preferred_element_type=jnp.float32)
        gh_ref[...] = out

    @pl.when(b == blocks - 1)
    def _():
        loss_ref[...] = loss_acc[...] * factor


def score(hidden, target, labels, chosen, offsets, table, factor):
    rows, features = hidden.shape
    blocks = rows // PB
    count = table.shape[0]
    pair, _, kb = chosen.shape
    half = NB // 2
    one = pl.Buffered(1)
    grid_spec = pltpu.PrefetchScalarGridSpec(
        num_scalar_prefetch=2,
        grid=(blocks,),
        in_specs=[
            pl.BlockSpec((PB, features), lambda b, *_: (b, 0)),
            pl.BlockSpec((PB, features), lambda b, *_: (b, 0)),
            pl.BlockSpec((1, 1, PB), lambda b, *_: (b, 0, 0)),
            pl.BlockSpec(table.shape, lambda b, *_: (0, 0, 0), pipeline_mode=one),
        ],
        out_specs=[
            pl.BlockSpec((PB, features), lambda b, *_: (b, 0)),
            pl.BlockSpec((8, 128), lambda b, *_: (0, 0)),
            pl.BlockSpec((2, 1, kb, half, PB), lambda b, *_: (0, b, 0, 0, 0)),
            pl.BlockSpec((PB, features), lambda b, *_: (b, 0)),
            pl.BlockSpec(memory_space=pltpu.SMEM),
        ],
        scratch_shapes=[
            pltpu.VMEM((PB, kb * NB), jnp.float32),
            pltpu.VMEM((8, 128), jnp.float32),
        ],
    )
    return pl.pallas_call(
        functools.partial(score_kernel, factor=factor),
        grid_spec=grid_spec,
        out_shape=(
            jax.ShapeDtypeStruct((rows, features), jnp.float32),
            jax.ShapeDtypeStruct((8, 128), jnp.float32),
            jax.ShapeDtypeStruct((2, blocks, kb, half, PB), jnp.bfloat16),
            jax.ShapeDtypeStruct((rows, features), jnp.bfloat16),
            jax.ShapeDtypeStruct((pair * blocks, count), jnp.int32),
        ),
        compiler_params=pltpu.CompilerParams(vmem_limit_bytes=60 << 20),
        name="score",
    )(chosen, offsets, hidden, target, labels.reshape(blocks, 1, PB), table)


MAIN = 384


def reduce_kernel(shares, narrow, slots, loss_in, out, loss_out, lists, wide, own, side, ready, landing, landing2,
                  landing3, landing4, landing5, parts, sums, load_sem, pair_send, pair_recv, s1, r1, s2, r2, s3, r3,
                  s4, r4, s5, r5, s6, r6, s7, r7, loss_send, loss_recv):
    x, y, z, c = where_am_i()
    users = x * NZ + z
    total = NX * NZ
    partner = device(x, y, z, 1 - c)
    xs = [device(lax.rem(x + d, NX), y, z, c) for d in range(1, NX)]
    ys = [device(x, lax.rem(y + d, NY), z, c) for d in range(1, NY)]
    zs = [device(x, y, lax.rem(z + d, NZ), c) for d in range(1, NZ)]
    others = [lax.rem(users + d, total) for d in range(1, total)]
    plane = [{"seq": y * 2 + c, "users": u} for u in others]
    blocks, kb = shares.shape[1:3]
    rows = own.shape[1]
    sub = rows // NY
    length = narrow.shape[0]

    def loss_round(k, base, me, peers):
        parts[base + me] = sums[...]
        return [push(sums, parts.at[base + me], loss_send.at[k + d], loss_recv.at[k + d], peer)
                for d, peer in enumerate(peers)]

    def loss_sum(copies, base, count):
        for copy in copies:
            copy.wait()
        added = parts[base]
        for i in range(1, count):
            added = added + parts[base + i]
        sums[...] = added

    sums[...] = loss_in[...]
    greet([partner] + ys + plane)
    losses = loss_round(0, 0, c, [partner])
    pair = [
        push(shares.at[1 - c], lists.at[pl.ds(c * blocks, blocks), pl.ds(0, kb)], pair_send.at[0], pair_recv.at[0], partner),
        push(narrow, wide.at[pl.ds(c * length, length)], pair_send.at[1], pair_recv.at[1], partner),
        pltpu.make_async_copy(shares.at[c], lists.at[pl.ds(c * blocks, blocks), pl.ds(0, kb)], load_sem.at[0]),
        pltpu.make_async_copy(narrow, wide.at[pl.ds(c * length, length)], load_sem.at[1]),
    ]
    for copy in pair[2:]:
        copy.start()
    for i in range(2 * blocks):
        lists[i, kb] = jnp.zeros(lists.shape[2:], lists.dtype)
    loss_sum(losses, 0, 2)
    for copy in pair:
        copy.wait()

    def half(ref, h):
        size = ref.shape[0] // 2
        return ref.at[pl.ds(h * size, size)]

    def add(dst, src):
        step = min(dst.shape[0], 64 if len(dst.shape) == 2 else 4)

        @pl.loop(0, dst.shape[0] // step)
        def _(i):
            here = pl.ds(pl.multiple_of(i * step, step), step)
            dst[here] += src[here]

    def tree(n, me, order, chunk, land, send_sems, recv_sems, up, down, fine=False):
        old = {}
        subs = len(order)
        for s in range(1, n // 2 + 2):
            ahead = n // 2 + 1 - s
            for i, j in enumerate(order):
                for d, to in ((1, up), (-1, down)):
                    ref = chunk(lax.rem(me + d * ahead + n, n), j)
                    if s > 1:
                        slot = ((s - 2) * subs + i) * 2 + (d < 0)
                        old[slot].wait_recv()
                        if s == 2:
                            add(half(ref, d < 0), half(land.at[slot], d < 0))
                        else:
                            add(ref, land.at[slot])
                    if ahead:
                        slot = ((s - 1) * subs + i) * 2 + (d < 0)
                        dst = land.at[slot]
                        if s == 1:
                            ref, dst = half(ref, d < 0), half(dst, d < 0)
                        old[slot] = push(ref, dst, send_sems.at[slot], recv_sems.at[slot], to)
                if fine and not ahead:
                    yield list(old.values())
            if ahead or not fine:
                yield list(old.values())

    def finish(steps):
        for copies in steps:
            pass
        return copies

    group = 4

    def produce(first, count, block):
        @pl.loop(0, count)
        def _(g):
            base = (first + g) * group
            lhs = []
            for i in range(group):
                k = block(base + i)
                lhs.append(jnp.concatenate([lists[b, slots[b, k]] for b in range(2 * blocks)], axis=1))
            found = jnp.dot(jnp.concatenate(lhs, axis=0), wide[...], preferred_element_type=jnp.float32)
            for i in range(group):
                own[base + i] = found[i * rows:(i + 1) * rows, :MAIN]
                for w in range(NY):
                    side[w, block(base + i)] = found[i * rows + w * sub:i * rows + (w + 1) * sub, MAIN:]

    def run(n1, n2, me1, me2, dev, block):
        per = n2 // group

        def make(*places):
            for place in places:
                produce(lax.rem(me1 + place + n1, n1) * per, per, block)

        reach = [n2 // 2] + [r for q in range(n2 // 2 - 1, 0, -1) for r in (q, -q)] + [0]
        main = tree(n1, me1, [lax.rem(me2 + r + n2, n2) for r in reach], lambda i1, j: own.at[i1 * n2 + j], landing,
                    s1, r1, dev(lax.rem(me1 + 1, n1), me2), dev(lax.rem(me1 + n1 - 1, n1), me2), fine=True)
        edge = tree(NY, y, range(NX), lambda i, j: side.at[i, pl.ds(j * NZ, NZ)], landing4, s6, r6, ys[0], ys[-1])
        second = tree(n2, me2, range(NY), lambda i, j: own.at[me1 * n2 + i, pl.ds(j * sub, sub)], landing2, s2, r2,
                      dev(me1, lax.rem(me2 + 1, n2)), dev(me1, lax.rem(me2 + n2 - 1, n2)))
        mine = own.at[me1 * n2 + me2]
        last = tree(NY, y, [0], lambda i, j: mine.at[pl.ds(i * sub, sub)], landing3, s3, r3, ys[0], ys[-1])
        make(n1 // 2)
        next(main)
        losses = loss_round(1, 2, y, ys)
        if n1 == NZ:
            make(3, -3)
            next(main)
            make(2, -2)
        make(1, -1, 0)
        next(edge)
        next(main)
        loss_sum(losses, 2, NY)
        losses = loss_round(4, 6, x, xs)
        next(edge)
        if n1 == NZ:
            next(main)
        sent = next(main)
        next(second)
        for _ in range(n2 // 2 - 1):
            next(main)
            next(main)
            next(second)
        next(main)
        loss_sum(losses, 6, NX)
        losses = loss_round(7, 10, z, zs)
        sent += finish(edge)
        direct = [push(side.at[y, u], landing5.at[d], s7.at[d], r7.at[d], peer)
                  for d, (u, peer) in enumerate(zip(others, plane))]
        sent += finish(second)
        sent += finish(last)
        ready[:, :MAIN] = mine[pl.ds(y * sub, sub)]
        for copy in direct:
            copy.wait_recv()
        found = side[y, users]
        for d in range(total - 1):
            found = found + landing5[d]
        ready[:, MAIN:] = found
        loss_sum(losses, 10, NZ)
        for copy in sent + direct:
            copy.wait_send()

    @pl.when(c == 0)
    def _():
        run(NZ, NX, z, x, lambda i1, i2: device(i2, y, i1, 0), lambda t: (t % NX) * NZ + t // NX)

    @pl.when(c == 1)
    def _():
        run(NX, NZ, x, z, lambda i1, i2: device(i1, y, i2, 1), lambda t: t)

    done = out.at[c, y]
    swaps = [push(ready, done, s4.at[0], r4.at[0], partner)]
    spread = [push(ready, done, s4.at[d], r4.at[d], peer) for d, peer in enumerate(ys, 1)]
    out[c, y] = ready[...]
    loss_out[...] = sums[:1, :1]
    for d, copy in enumerate(spread, 1):
        copy.wait_recv()
        ref = out.at[c, lax.rem(y + NY - d, NY)]
        swaps.append(push(ref, ref, s5.at[d - 1], r5.at[d - 1], partner))
    for copy in swaps:
        copy.wait_recv()
    for copy in spread + swaps:
        copy.wait_send()


def reduce_rows(shares, narrow, slots, loss):
    pair, blocks, kb, half, width = shares.shape
    length, features = narrow.shape
    total = NX * NZ
    sub = half // NY
    edge = features - MAIN
    dma = pltpu.SemaphoreType.DMA
    f32 = jnp.float32
    anywhere = pl.BlockSpec(memory_space=pl.ANY)
    vmem = pl.BlockSpec(memory_space=pltpu.VMEM)
    out, loss = pl.pallas_call(
        reduce_kernel,
        in_specs=[anywhere, anywhere, pl.BlockSpec(memory_space=pltpu.SMEM), vmem],
        out_specs=[vmem, vmem],
        out_shape=(jax.ShapeDtypeStruct((2, NY, sub, features), f32), jax.ShapeDtypeStruct((1, 1), f32)),
        scratch_shapes=[
            pltpu.VMEM((pair * blocks, kb + 1, half, width), shares.dtype),
            pltpu.VMEM((pair * length, features), narrow.dtype),
            pltpu.VMEM((total, half, MAIN), f32),
            pltpu.VMEM((NY, total, sub, edge), f32),
            pltpu.VMEM((sub, features), f32),
            pltpu.VMEM((32, half, MAIN), f32),
            pltpu.VMEM((32, sub, MAIN), f32),
            pltpu.VMEM((4, sub, MAIN), f32),
            pltpu.VMEM((16, NZ, sub, edge), f32),
            pltpu.VMEM((total - 1, sub, edge), f32),
            pltpu.VMEM((2 + NY + NX + NZ,) + loss.shape, f32),
            pltpu.VMEM(loss.shape, f32),
            dma((2,)), dma((2,)), dma((2,)),
            dma((32,)), dma((32,)), dma((32,)), dma((32,)), dma((4,)), dma((4,)),
            dma((4,)), dma((4,)), dma((3,)), dma((3,)), dma((16,)), dma((16,)), dma((total - 1,)), dma((total - 1,)),
            dma((14,)), dma((14,)),
        ],
        compiler_params=pltpu.CompilerParams(collective_id=1, has_side_effects=True, vmem_limit_bytes=63 << 20),
        name="reduce",
    )(shares, narrow, slots, loss)
    return out.reshape(2 * half, features), loss.reshape(())


def per_device(hidden, target, pool_table, pool_items, labels, chosen, offsets):
    user_count = lax.axis_size("users")
    factor = 1.0 / (user_count * (offsets.shape[1] - 1))
    table, both = gather(pool_table, pool_items, chosen[0])
    grad_hidden, loss, shares, narrow, slots = score(
        hidden[0], target[0], labels[0], both, offsets[0], table, factor
    )
    grad_table, loss_total = reduce_rows(shares, narrow, slots, loss)
    return (loss_total, grad_hidden[None], grad_table)


def solution(mesh):
    return jax.shard_map(
        per_device,
        mesh=mesh,
        in_specs=(
            P("users", "seq", None),
            P("users", "seq", None),
            P("users", None),
            P("users"),
            P("users", "seq"),
            P("users", "seq", None),
            P("users", None),
        ),
        out_specs=(P(), P("users", "seq", None), P("users", None)),
        check_vma=False,
    )
```

time: 160 us -> 149 us (0.931)
  Pallas kernels: 154 us -> 145 us
    pallas_call x1, Pallas kernels: 86.5 us -> 80 us  [reduce_rows(): pl.pallas_call(reduce_kernel, in_specs=[anywhere, anywhere, pl.BlockSpec(...]
    pallas_call x1, Pallas kernels: 48.3 us -> 46 us  [gather(): pl.pallas_call(gather_kernel, in_specs=[pl.BlockSpec(memory_space=pltpu.V...]
where the time goes in v3:
time: 149 us
  Pallas kernels  145 us (97%)
  between operations  2.4 us (2%)
  local copies, waits for them, and re-layouts  1.87 us (1%)
    pallas_call x1, Pallas kernels, reduce_rows(): pl.pallas_call(reduce_kernel, in_specs=[anywhere, anywhere, pl.BlockSpec(...  80 us
    pallas_call x1, Pallas kernels, gather(): pl.pallas_call(gather_kernel, in_specs=[pl.BlockSpec(memory_space=pltpu.V...  46 us
    pallas_call x1, Pallas kernels, score(): pl.pallas_call(functools.partial(score_kernel, factor=factor), grid_spec=...  19.2 us

profile of v3, /device:TPU:1, one launch (start us, length us, event | category | flops | bytes accessed | tf_op | source)
XLA Modules:
  0.0 149.4 jit_solution(6839420083769206850)
XLA Ops:
  0.6 46.0 %gather.1 = (bf16[32,272,512]{2,1,0:T(8,128)(2,1)}, s32[2,8,8]{2,1,0:T(8,128)}) custom-call(bf16[256,512]{1,0:T(8,128)(2,1)} %shard.1, s32[1,256]{1,0:T(1,128)} %bitcast.14, s32[8,8]{1,0:T(8,128)} %bitcast.13), custom_call_target="tpu_custom_call" | custom-call | tf_op jit(solution)/shard_map/gather/pallas_call | solution.py:135
  46.6 19.2 %score.1 = (f32[1024,512]{1,0:T(8,128)}, f32[8,128]{1,0:T(8,128)}, bf16[2,8,8,128,128]{4,3,2,1,0:T(8,128)(2,1)}, bf16[1024,512]{1,0:T(8,128)(2,1)}, s32[16,32]{1,0:T(8,128)}) custom-call(s32[2,8,8]{2,1,0:T(8,128)} %get-tuple-element.12.chosen_s, s32[5]{0:T(128)} %bitcast.15, f32[1024,512]{1,0:T(8,128)} %bitcast.9, bf16[1024,512]{1,0:T(8,128)(2,1)} %bitcast.10, ...), custom_call_target="tpu_custom_call" | custom-call | tf_op jit(solution)/shard_map/score/pallas_call | solution.py:269
  65.8 80.0 %reduce.1 = (f32[2,4,32,512]{3,2,1,0:T(8,128)}, f32[1,1]{1,0:T(1,128)}) custom-call(bf16[2,8,8,128,128]{4,3,2,1,0:T(8,128)(2,1)} %get-tuple-element.14.shares, bf16[1024,512]{1,0:T(8,128)(2,1)} %get-tuple-element.15.narrow, s32[16,32]{1,0:T(8,128)} %get-tuple-element.16.slots, f32[8,128]{1,0:T(8,128)} %get-tuple-element.17.loss_in), custom_call_target="tpu_custom_call" | custom-call | tf_op jit(solution)/shard_map/reduce/pallas_call | solution.py:481
  146.4 1.9 %copy.13 = f32[256,512]{1,0:T(8,128)} copy(f32[256,512]{1,0:T(8,128)} %bitcast.11) | data formatting | bytes 1048576

commit v4 on v3

--- a/solution.py
+++ b/solution.py
@@ -151,69 +151,72 @@
 
 NB = 256
 PB = 128
+TOGETHER = 2
 
 
 def score_kernel(chosen_s, offsets_s, hidden_ref, target_ref, labels_ref, table_ref,
                  gh_ref, loss_ref, shares_ref, narrow_ref, slots_ref, scores, loss_acc, *, factor):
-    b = pl.program_id(0)
-    blocks = pl.num_programs(0)
-    pair, _, kb = chosen_s.shape
+    step = pl.program_id(0)
+    steps = pl.num_programs(0)
+    pair, blocks, kb = chosen_s.shape
     count = table_ref.shape[0]
     hists = offsets_s.shape[0] - 1
     seq = lax.axis_index("seq")
     core = seq % 2
-    base = (seq * blocks + b) * PB
-
-    for other in range(pair):
-        for k in range(count):
-            slots_ref[other * blocks + b, k] = kb
-    for other in range(pair):
-        for j in range(kb):
-            slots_ref[other * blocks + b, chosen_s[other, b, j]] = j
-
-    @pl.when(b == 0)
+
+    for u in range(TOGETHER):
+        b = step * TOGETHER + u
+        for other in range(pair):
+            for k in range(count):
+                slots_ref[other * blocks + b, k] = kb
+        for other in range(pair):
+            for j in range(kb):
+                slots_ref[other * blocks + b, chosen_s[other, b, j]] = j
+
+    @pl.when(step == 0)
     def _():
         loss_acc[...] = jnp.zeros_like(loss_acc)
 
-    live = base < offsets_s[hists]
-    narrow = hidden_ref[...].astype(jnp.bfloat16)
-    narrow_ref[...] = narrow
+    first = (seq * blocks + step * TOGETHER) * PB
+    live = first < offsets_s[hists]
+    narrow_ref[...] = hidden_ref[...].astype(jnp.bfloat16)
 
     @pl.when(jnp.logical_not(live))
     def _():
         gh_ref[...] = jnp.zeros_like(gh_ref)
         shares_ref[...] = jnp.zeros_like(shares_ref)
 
-    @pl.when(live)
-    def _():
-        target_wide = target_ref[...].astype(jnp.float32)
-        positive = jnp.sum(narrow.astype(jnp.float32) * target_wide, axis=1, keepdims=True)
-        labels = jnp.broadcast_to(labels_ref[0].astype(jnp.float32), (PB, PB)).T[:, :1]
-        positions = base + lax.broadcasted_iota(jnp.int32, (PB, 1), 0)
+    def look(u):
+        b = step * TOGETHER + u
+        rows = pl.ds(u * PB, PB)
+        narrow = hidden_ref[rows].astype(jnp.bfloat16)
+        positive = jnp.sum(narrow.astype(jnp.float32) * target_ref[rows].astype(jnp.float32), axis=1, keepdims=True)
+        labels = jnp.broadcast_to(labels_ref[u].astype(jnp.float32), (PB, PB)).T[:, :1]
+        top = jnp.full((PB, 128), -1e30, jnp.float32)
+        for j in range(kb):
+            k = chosen_s[core, b, j]
+            digits = table_ref[k, NB:][:1].astype(jnp.float32)
+            items = digits[:, :NB] * 128.0 + digits[:, NB:]
+            raw = lax.dot_general(narrow, table_ref[k, :NB], (((1,), (1,)), ((), ())),
+                                  preferred_element_type=jnp.float32)
+            masked = jnp.where(items == labels, -1e30, raw)
+            scores[u, :, j * NB:(j + 1) * NB] = masked
+            for i in range(NB // 128):
+                top = jnp.maximum(top, masked[:, i * 128:(i + 1) * 128])
+        return positive, jnp.maximum(positive, jnp.max(top, axis=1, keepdims=True))
+
+    def weigh(u, positive, peak):
+        positions = first + u * PB + lax.broadcasted_iota(jnp.int32, (PB, 1), 0)
         weights = jnp.zeros((PB, 1), jnp.float32)
         for h in range(hists):
             start, finish = offsets_s[h], offsets_s[h + 1]
             length = jnp.broadcast_to(finish - start, (PB, 1)).astype(jnp.float32)
             inside = (positions >= start) & (positions < finish)
             weights = weights + jnp.where(inside, 1.0 / length, 0.0)
-
-        top = jnp.full((PB, 128), -1e30, jnp.float32)
-        for j in range(kb):
-            k = chosen_s[core, b, j]
-            rows = table_ref[k, :NB]
-            digits = table_ref[k, NB:][:1].astype(jnp.float32)
-            items = digits[:, :NB] * 128.0 + digits[:, NB:]
-            raw = lax.dot_general(narrow, rows, (((1,), (1,)), ((), ())),
-                                  preferred_element_type=jnp.float32)
-            masked = jnp.where(items == labels, -1e30, raw)
-            scores[:, j * NB:(j + 1) * NB] = masked
-            for i in range(NB // 128):
-                top = jnp.maximum(top, masked[:, i * 128:(i + 1) * 128])
-        peak = jnp.maximum(positive, jnp.max(top, axis=1, keepdims=True))
         added = jnp.zeros((PB, 128), jnp.float32)
         for j in range(kb):
-            each = jnp.exp(scores[:, j * NB:(j + 1) * NB] - peak)
-            scores[:, j * NB:(j + 1) * NB] = each
+            each = jnp.exp(scores[u, :, j * NB:(j + 1) * NB] - peak)
+            scores[u, :, j * NB:(j + 1) * NB] = each
             for i in range(NB // 128):
                 added = added + each[:, i * 128:(i + 1) * 128]
         pos_exp = jnp.exp(positive - peak)
@@ -221,19 +224,30 @@
         cross = peak + jnp.log(totals) - positive
         loss_acc[...] += jnp.broadcast_to(jnp.sum(weights * cross, axis=0, keepdims=True), loss_acc.shape)
         coeff = weights * factor
-        scale = coeff / totals
-        pos_grad = coeff * (pos_exp / totals - 1.0)
-        out = pos_grad * target_wide
+        return coeff / totals, coeff * (pos_exp / totals - 1.0)
+
+    def pull(u, scale, pos_grad):
+        b = step * TOGETHER + u
+        rows = pl.ds(u * PB, PB)
+        out = pos_grad * target_ref[rows].astype(jnp.float32)
         for j in range(kb):
             k = chosen_s[core, b, j]
-            g = (scores[:, j * NB:(j + 1) * NB] * scale).astype(jnp.bfloat16)
+            g = (scores[u, :, j * NB:(j + 1) * NB] * scale).astype(jnp.bfloat16)
             gt = g.T
-            shares_ref[0, 0, j] = gt[:128]
-            shares_ref[1, 0, j] = gt[128:]
+            shares_ref[0, u, j] = gt[:PB]
+            shares_ref[1, u, j] = gt[PB:]
             out = out + jnp.dot(g, table_ref[k, :NB], preferred_element_type=jnp.float32)
-        gh_ref[...] = out
-
-    @pl.when(b == blocks - 1)
+        gh_ref[rows] = out
+
+    @pl.when(live)
+    def _():
+        seen = [look(0)]
+        for u in range(TOGETHER):
+            if u + 1 < TOGETHER:
+                seen.append(look(u + 1))
+            pull(u, *weigh(u, *seen[u]))
+
+    @pl.when(step == steps - 1)
     def _():
         loss_ref[...] = loss_acc[...] * factor
 
@@ -247,22 +261,22 @@
     one = pl.Buffered(1)
     grid_spec = pltpu.PrefetchScalarGridSpec(
         num_scalar_prefetch=2,
-        grid=(blocks,),
+        grid=(blocks // TOGETHER,),
         in_specs=[
-            pl.BlockSpec((PB, features), lambda b, *_: (b, 0)),
-            pl.BlockSpec((PB, features), lambda b, *_: (b, 0)),
-            pl.BlockSpec((1, 1, PB), lambda b, *_: (b, 0, 0)),
+            pl.BlockSpec((TOGETHER * PB, features), lambda b, *_: (b, 0)),
+            pl.BlockSpec((TOGETHER * PB, features), lambda b, *_: (b, 0)),
+            pl.BlockSpec((TOGETHER, 1, PB), lambda b, *_: (b, 0, 0)),
             pl.BlockSpec(table.shape, lambda b, *_: (0, 0, 0), pipeline_mode=one),
         ],
         out_specs=[
-            pl.BlockSpec((PB, features), lambda b, *_: (b, 0)),
+            pl.BlockSpec((TOGETHER * PB, features), lambda b, *_: (b, 0)),
             pl.BlockSpec((8, 128), lambda b, *_: (0, 0)),
-            pl.BlockSpec((2, 1, kb, half, PB), lambda b, *_: (0, b, 0, 0, 0)),
-            pl.BlockSpec((PB, features), lambda b, *_: (b, 0)),
+            pl.BlockSpec((2, TOGETHER, kb, half, PB), lambda b, *_: (0, b, 0, 0, 0)),
+            pl.BlockSpec((TOGETHER * PB, features), lambda b, *_: (b, 0)),
             pl.BlockSpec(memory_space=pltpu.SMEM),
         ],
         scratch_shapes=[
-            pltpu.VMEM((PB, kb * NB), jnp.float32),
+            pltpu.VMEM((TOGETHER, PB, kb * NB), jnp.float32),
             pltpu.VMEM((8, 128), jnp.float32),
         ],
     )
@@ -284,7 +298,7 @@
 MAIN = 384
 
 
-def reduce_kernel(shares, narrow, slots, loss_in, out, loss_out, lists, wide, own, side, ready, landing, landing2,
+def reduce_kernel(shares, narrow, slots, loss_in, out, loss_out, lists, wide, own, side, ready, last, landing, landing2,
                   landing3, landing4, landing5, parts, sums, load_sem, pair_send, pair_recv, s1, r1, s2, r2, s3, r3,
                   s4, r4, s5, r5, s6, r6, s7, r7, loss_send, loss_recv):
     x, y, z, c = where_am_i()
@@ -374,6 +388,10 @@
             pass
         return copies
 
+    def share(ref, start, width, base):
+        done = out.at[c, y, :, pl.ds(start, width)]
+        return [push(ref, done, s4.at[base + d], r4.at[base + d], peer) for d, peer in enumerate([partner] + ys)]
+
     group = 4
 
     def produce(first, count, block):
@@ -404,7 +422,6 @@
         second = tree(n2, me2, range(NY), lambda i, j: own.at[me1 * n2 + i, pl.ds(j * sub, sub)], landing2, s2, r2,
                       dev(me1, lax.rem(me2 + 1, n2)), dev(me1, lax.rem(me2 + n2 - 1, n2)))
         mine = own.at[me1 * n2 + me2]
-        last = tree(NY, y, [0], lambda i, j: mine.at[pl.ds(i * sub, sub)], landing3, s3, r3, ys[0], ys[-1])
         make(n1 // 2)
         next(main)
         losses = loss_round(1, 2, y, ys)
@@ -433,16 +450,21 @@
         direct = [push(side.at[y, u], landing5.at[d], s7.at[d], r7.at[d], peer)
                   for d, (u, peer) in enumerate(zip(others, plane))]
         sent += finish(second)
-        sent += finish(last)
-        ready[:, :MAIN] = mine[pl.ds(y * sub, sub)]
+        trade = [push(mine.at[pl.ds(lax.rem(y + d, NY) * sub, sub)], landing3.at[d - 1], s3.at[d - 1], r3.at[d - 1], peer)
+                 for d, peer in enumerate(ys, 1)]
+        for copy in trade:
+            copy.wait_recv()
+        ready[...] = mine[pl.ds(y * sub, sub)] + landing3[0] + landing3[1] + landing3[2]
+        sent += share(ready, 0, MAIN, 0)
         for copy in direct:
             copy.wait_recv()
         found = side[y, users]
         for d in range(total - 1):
             found = found + landing5[d]
-        ready[:, MAIN:] = found
+        last[...] = found
+        sent += share(last, MAIN, found.shape[1], 4)
         loss_sum(losses, 10, NZ)
-        for copy in sent + direct:
+        for copy in sent + direct + trade:
             copy.wait_send()
 
     @pl.when(c == 0)
@@ -453,19 +475,20 @@
     def _():
         run(NX, NZ, x, z, lambda i1, i2: device(i1, y, i2, 1), lambda t: t)
 
-    done = out.at[c, y]
-    swaps = [push(ready, done, s4.at[0], r4.at[0], partner)]
-    spread = [push(ready, done, s4.at[d], r4.at[d], peer) for d, peer in enumerate(ys, 1)]
-    out[c, y] = ready[...]
+    out[c, y, :, :MAIN] = ready[...]
+    out[c, y, :, MAIN:] = last[...]
     loss_out[...] = sums[:1, :1]
-    for d, copy in enumerate(spread, 1):
-        copy.wait_recv()
-        ref = out.at[c, lax.rem(y + NY - d, NY)]
-        swaps.append(push(ref, ref, s5.at[d - 1], r5.at[d - 1], partner))
-    for copy in swaps:
-        copy.wait_recv()
-    for copy in spread + swaps:
-        copy.wait_send()
+    passed = []
+    for base, start, width in ((0, 0, MAIN), (4, MAIN, last.shape[1])):
+        for d in range(1, NY):
+            ref = out.at[c, lax.rem(y + NY - d, NY), :, pl.ds(start, width)]
+            pltpu.make_async_copy(ref, ref, r4.at[base + d]).wait()
+            passed.append(push(ref, ref, s5.at[len(passed)], r5.at[len(passed)], partner))
+    for base, start, width in ((0, 0, MAIN), (4, MAIN, last.shape[1])):
+        ref = out.at[c, y, :, pl.ds(start, width)]
+        pltpu.make_async_copy(ref, ref, r4.at[base]).wait()
+    for copy in passed:
+        copy.wait()
 
 
 def reduce_rows(shares, narrow, slots, loss):
@@ -488,7 +511,8 @@
             pltpu.VMEM((pair * length, features), narrow.dtype),
             pltpu.VMEM((total, half, MAIN), f32),
             pltpu.VMEM((NY, total, sub, edge), f32),
-            pltpu.VMEM((sub, features), f32),
+            pltpu.VMEM((sub, MAIN), f32),
+            pltpu.VMEM((sub, edge), f32),
             pltpu.VMEM((32, half, MAIN), f32),
             pltpu.VMEM((32, sub, MAIN), f32),
             pltpu.VMEM((4, sub, MAIN), f32),
@@ -498,7 +522,7 @@
             pltpu.VMEM(loss.shape, f32),
             dma((2,)), dma((2,)), dma((2,)),
             dma((32,)), dma((32,)), dma((32,)), dma((32,)), dma((4,)), dma((4,)),
-            dma((4,)), dma((4,)), dma((3,)), dma((3,)), dma((16,)), dma((16,)), dma((total - 1,)), dma((total - 1,)),
+            dma((8,)), dma((8,)), dma((6,)), dma((6,)), dma((16,)), dma((16,)), dma((total - 1,)), dma((total - 1,)),
             dma((14,)), dma((14,)),
         ],
         compiler_params=pltpu.CompilerParams(collective_id=1, has_side_effects=True, vmem_limit_bytes=63 << 20),

time: 149 us -> 146 us (0.980)
  Pallas kernels: 145 us -> 141 us
    pallas_call x1, Pallas kernels: 19.2 us -> 13.5 us  [score(): pl.pallas_call(functools.partial(score_kernel, factor=factor), grid_spec=...]
where the time goes in v4:
time: 146 us; the launch traced here: 145 us
  Pallas kernels  141 us (97%)
  between operations  2.4 us (2%)
  local copies, waits for them, and re-layouts  1.87 us (1%)
    pallas_call x1, Pallas kernels, reduce_rows(): pl.pallas_call(reduce_kernel, in_specs=[anywhere, anywhere, pl.BlockSpec(...  81.3 us
    pallas_call x1, Pallas kernels, gather(): pl.pallas_call(gather_kernel, in_specs=[pl.BlockSpec(memory_space=pltpu.V...  46 us
    pallas_call x1, Pallas kernels, score(): pl.pallas_call(functools.partial(score_kernel, factor=factor), grid_spec=...  13.5 us

profile of v4, /device:TPU:1, one launch (start us, length us, event | category | flops | bytes accessed | tf_op | source)
XLA Modules:
  0.0 145.0 jit_solution(16990835031067525223)
XLA Ops:
  0.6 46.0 %gather.1 = (bf16[32,272,512]{2,1,0:T(8,128)(2,1)}, s32[2,8,8]{2,1,0:T(8,128)}) custom-call(bf16[256,512]{1,0:T(8,128)(2,1)} %shard.1, s32[1,256]{1,0:T(1,128)} %bitcast.14, s32[8,8]{1,0:T(8,128)} %bitcast.13), custom_call_target="tpu_custom_call" | custom-call | tf_op jit(solution)/shard_map/gather/pallas_call | solution.py:135
  46.6 13.5 %score.1 = (f32[1024,512]{1,0:T(8,128)}, f32[8,128]{1,0:T(8,128)}, bf16[2,8,8,128,128]{4,3,2,1,0:T(8,128)(2,1)}, bf16[1024,512]{1,0:T(8,128)(2,1)}, s32[16,32]{1,0:T(8,128)}) custom-call(s32[2,8,8]{2,1,0:T(8,128)} %get-tuple-element.12.chosen_s, s32[5]{0:T(128)} %bitcast.15, f32[1024,512]{1,0:T(8,128)} %bitcast.9, bf16[1024,512]{1,0:T(8,128)(2,1)} %bitcast.10, ...), custom_call_target="tpu_custom_call" | custom-call | tf_op jit(solution)/shard_map/score/pallas_call | solution.py:283
  60.1 81.3 %reduce.1 = (f32[2,4,32,512]{3,2,1,0:T(8,128)}, f32[1,1]{1,0:T(1,128)}) custom-call(bf16[2,8,8,128,128]{4,3,2,1,0:T(8,128)(2,1)} %get-tuple-element.14.shares, bf16[1024,512]{1,0:T(8,128)(2,1)} %get-tuple-element.15.narrow, s32[16,32]{1,0:T(8,128)} %get-tuple-element.16.slots, f32[8,128]{1,0:T(8,128)} %get-tuple-element.17.loss_in), custom_call_target="tpu_custom_call" | custom-call | tf_op jit(solution)/shard_map/reduce/pallas_call | solution.py:504
  142.0 1.9 %copy.13 = f32[256,512]{1,0:T(8,128)} copy(f32[256,512]{1,0:T(8,128)} %bitcast.11) | data formatting | bytes 1048576

commit v5 on v4

--- a/solution.py
+++ b/solution.py
@@ -39,7 +39,7 @@
     users = x * NZ + z
     total = NX * NZ
     rows = shard.shape[0]
-    cut = rows * 3 // 8
+    cut = rows // 2
     partner = device(x, y, z, 1 - c)
 
     whole[:rows] = shard[...]
@@ -49,7 +49,7 @@
     rows = rows + EXTRA
 
     greet([partner] + [device(lax.rem(x + d, NX), y, z, c) for d in range(1, NX)]
-          + [device(x, y, lax.rem(z + d, NZ), c) for d in (1, 2, NZ - 2, NZ - 1)])
+          + [device(x, y, lax.rem(z + d, NZ), c) for d in (1, NZ - 1)])
     mine = pltpu.make_async_copy(whole, table.at[users], local_sem.at[0])
     mine.start()
     mine_chosen = pltpu.make_async_copy(chosen, both.at[c], local_sem.at[1])
@@ -111,8 +111,8 @@
         pltpu.make_async_copy(rest, rest, partner_recv).wait()
 
     across = [(1, 0, 1, None), (1, 0, -1, None), (1, 0, 2, None)]
-    along = [(1, 0, 1, None), (1, 0, -1, None), (1, 0, 2, None), (1, 0, -2, None),
-             (2, 2, 1, None), (2, -2, -1, None), (2, 2, 2, 0), (2, -2, -2, 1)]
+    along = [(1, 0, 1, None), (1, 0, -1, None), (2, 1, 1, None), (2, -1, -1, None),
+             (3, 2, 1, None), (3, -2, -1, None), (4, 3, 1, 0), (4, -3, -1, 1)]
 
     @pl.when(c == 0)
     def _():

time: 146 us -> 143 us (0.979)
  Pallas kernels: 141 us -> 139 us
    pallas_call x1, Pallas kernels: 13.5 us -> 17.2 us  [score(): pl.pallas_call(functools.partial(score_kernel, factor=factor), grid_spec=...]
    pallas_call x1, Pallas kernels: 81.3 us -> 77.7 us  [reduce_rows(): pl.pallas_call(reduce_kernel, in_specs=[anywhere, anywhere, pl.BlockSpec(...]
    pallas_call x1, Pallas kernels: 46 us -> 43.9 us  [gather(): pl.pallas_call(gather_kernel, in_specs=[pl.BlockSpec(memory_space=pltpu.V...]
where the time goes in v5:
time: 143 us
  Pallas kernels  139 us (97%)
  between operations  2.4 us (2%)
  local copies, waits for them, and re-layouts  1.87 us (1%)
    pallas_call x1, Pallas kernels, reduce_rows(): pl.pallas_call(reduce_kernel, in_specs=[anywhere, anywhere, pl.BlockSpec(...  77.7 us
    pallas_call x1, Pallas kernels, gather(): pl.pallas_call(gather_kernel, in_specs=[pl.BlockSpec(memory_space=pltpu.V...  43.9 us
    pallas_call x1, Pallas kernels, score(): pl.pallas_call(functools.partial(score_kernel, factor=factor), grid_spec=...  17.2 us

profile of v5, /device:TPU:1, one launch (start us, length us, event | category | flops | bytes accessed | tf_op | source)
XLA Modules:
  0.0 143.1 jit_solution(6473240285378932115)
XLA Ops:
  0.6 43.9 %gather.1 = (bf16[32,272,512]{2,1,0:T(8,128)(2,1)}, s32[2,8,8]{2,1,0:T(8,128)}) custom-call(bf16[256,512]{1,0:T(8,128)(2,1)} %shard.1, s32[1,256]{1,0:T(1,128)} %bitcast.14, s32[8,8]{1,0:T(8,128)} %bitcast.13), custom_call_target="tpu_custom_call" | custom-call | tf_op jit(solution)/shard_map/gather/pallas_call | solution.py:135
  44.5 17.2 %score.1 = (f32[1024,512]{1,0:T(8,128)}, f32[8,128]{1,0:T(8,128)}, bf16[2,8,8,128,128]{4,3,2,1,0:T(8,128)(2,1)}, bf16[1024,512]{1,0:T(8,128)(2,1)}, s32[16,32]{1,0:T(8,128)}) custom-call(s32[2,8,8]{2,1,0:T(8,128)} %get-tuple-element.12.chosen_s, s32[5]{0:T(128)} %bitcast.15, f32[1024,512]{1,0:T(8,128)} %bitcast.9, bf16[1024,512]{1,0:T(8,128)(2,1)} %bitcast.10, ...), custom_call_target="tpu_custom_call" | custom-call | tf_op jit(solution)/shard_map/score/pallas_call | solution.py:283
  61.8 77.7 %reduce.1 = (f32[2,4,32,512]{3,2,1,0:T(8,128)}, f32[1,1]{1,0:T(1,128)}) custom-call(bf16[2,8,8,128,128]{4,3,2,1,0:T(8,128)(2,1)} %get-tuple-element.14.shares, bf16[1024,512]{1,0:T(8,128)(2,1)} %get-tuple-element.15.narrow, s32[16,32]{1,0:T(8,128)} %get-tuple-element.16.slots, f32[8,128]{1,0:T(8,128)} %get-tuple-element.17.loss_in), custom_call_target="tpu_custom_call" | custom-call | tf_op jit(solution)/shard_map/reduce/pallas_call | solution.py:504
  140.1 1.9 %copy.13 = f32[256,512]{1,0:T(8,128)} copy(f32[256,512]{1,0:T(8,128)} %bitcast.11) | data formatting | bytes 1048576

commit v6 on v5

--- a/solution.py
+++ b/solution.py
@@ -329,18 +329,20 @@
         sums[...] = added
 
     sums[...] = loss_in[...]
+    loads = [
+        pltpu.make_async_copy(shares.at[c], lists.at[pl.ds(c * blocks, blocks), pl.ds(0, kb)], load_sem.at[0]),
+        pltpu.make_async_copy(narrow, wide.at[pl.ds(c * length, length)], load_sem.at[1]),
+    ]
+    for copy in loads:
+        copy.start()
+    for i in range(2 * blocks):
+        lists[i, kb] = jnp.zeros(lists.shape[2:], lists.dtype)
     greet([partner] + ys + plane)
     losses = loss_round(0, 0, c, [partner])
     pair = [
         push(shares.at[1 - c], lists.at[pl.ds(c * blocks, blocks), pl.ds(0, kb)], pair_send.at[0], pair_recv.at[0], partner),
         push(narrow, wide.at[pl.ds(c * length, length)], pair_send.at[1], pair_recv.at[1], partner),
-        pltpu.make_async_copy(shares.at[c], lists.at[pl.ds(c * blocks, blocks), pl.ds(0, kb)], load_sem.at[0]),
-        pltpu.make_async_copy(narrow, wide.at[pl.ds(c * length, length)], load_sem.at[1]),
-    ]
-    for copy in pair[2:]:
-        copy.start()
-    for i in range(2 * blocks):
-        lists[i, kb] = jnp.zeros(lists.shape[2:], lists.dtype)
+    ] + loads
     loss_sum(losses, 0, 2)
     for copy in pair:
         copy.wait()

time: 143 us -> 144 us (level)
  no operation moved by 1% of the time
where the time goes in v6:
time: 144 us; the launch traced here: 143 us
  Pallas kernels  139 us (97%)
  between operations  2.4 us (2%)
  local copies, waits for them, and re-layouts  1.87 us (1%)
    pallas_call x1, Pallas kernels, reduce_rows(): pl.pallas_call(reduce_kernel, in_specs=[anywhere, anywhere, pl.BlockSpec(...  77.9 us
    pallas_call x1, Pallas kernels, gather(): pl.pallas_call(gather_kernel, in_specs=[pl.BlockSpec(memory_space=pltpu.V...  43.9 us
    pallas_call x1, Pallas kernels, score(): pl.pallas_call(functools.partial(score_kernel, factor=factor), grid_spec=...  17.2 us

profile of v6, /device:TPU:1, one launch (start us, length us, event | category | flops | bytes accessed | tf_op | source)
XLA Modules:
  0.0 143.3 jit_solution(10744590736391554494)
XLA Ops:
  0.6 43.9 %gather.1 = (bf16[32,272,512]{2,1,0:T(8,128)(2,1)}, s32[2,8,8]{2,1,0:T(8,128)}) custom-call(bf16[256,512]{1,0:T(8,128)(2,1)} %shard.1, s32[1,256]{1,0:T(1,128)} %bitcast.14, s32[8,8]{1,0:T(8,128)} %bitcast.13), custom_call_target="tpu_custom_call" | custom-call | tf_op jit(solution)/shard_map/gather/pallas_call | solution.py:135
  44.5 17.2 %score.1 = (f32[1024,512]{1,0:T(8,128)}, f32[8,128]{1,0:T(8,128)}, bf16[2,8,8,128,128]{4,3,2,1,0:T(8,128)(2,1)}, bf16[1024,512]{1,0:T(8,128)(2,1)}, s32[16,32]{1,0:T(8,128)}) custom-call(s32[2,8,8]{2,1,0:T(8,128)} %get-tuple-element.12.chosen_s, s32[5]{0:T(128)} %bitcast.15, f32[1024,512]{1,0:T(8,128)} %bitcast.9, bf16[1024,512]{1,0:T(8,128)(2,1)} %bitcast.10, ...), custom_call_target="tpu_custom_call" | custom-call | tf_op jit(solution)/shard_map/score/pallas_call | solution.py:283
  61.8 77.9 %reduce.1 = (f32[2,4,32,512]{3,2,1,0:T(8,128)}, f32[1,1]{1,0:T(1,128)}) custom-call(bf16[2,8,8,128,128]{4,3,2,1,0:T(8,128)(2,1)} %get-tuple-element.14.shares, bf16[1024,512]{1,0:T(8,128)(2,1)} %get-tuple-element.15.narrow, s32[16,32]{1,0:T(8,128)} %get-tuple-element.16.slots, f32[8,128]{1,0:T(8,128)} %get-tuple-element.17.loss_in), custom_call_target="tpu_custom_call" | custom-call | tf_op jit(solution)/shard_map/reduce/pallas_call | solution.py:506
  140.3 1.9 %copy.13 = f32[256,512]{1,0:T(8,128)} copy(f32[256,512]{1,0:T(8,128)} %bitcast.11) | data formatting | bytes 1048576
